TPU v7x, 32 devices: a whole 2x2x4 slice. The times are simulated.
32 devices in a mesh: dp: 8 (over z, y), tensor: 4 (over x, core).
Axes of the slice: x: 2, y: 2, z: 4, core: 2. Of those that a mesh axis runs over, the one named last changes fastest.
Arguments:
- inputs: bfloat16 [16384, 768], P('dp'), may hold values from -6 to 6
- first_values: bfloat16 [16384, 384], P('dp'), may hold values from -6 to 6
- piece_start: int32 [16, 2], P('dp'), may hold values from 0 to 896, as said below
- piece_length: int32 [16, 2], P('dp'), may hold values from 128 to 256, as said below
- cotangent: bfloat16 [16384, 768], P('dp'), may hold values from -6 to 6
- pre_attn_gain: float32 [768], replicated, may hold values from 0.5 to 1.5
- pre_attn_bias: float32 [768], replicated, may hold values from -1.5 to 1.5
- w_query: bfloat16 [768, 768], P(None, 'tensor'), may hold values from -0.21875 to 0.21875
- w_key: bfloat16 [768, 768], P(None, 'tensor'), may hold values from -0.21875 to 0.21875
- w_value: bfloat16 [768, 384], replicated, may hold values from -0.21875 to 0.21875
- w_out: bfloat16 [768, 768], P('tensor'), may hold values from -1.75 to 1.75
- pre_mlp_gain: float32 [768], replicated, may hold values from 0.5 to 1.5
- pre_mlp_bias: float32 [768], replicated, may hold values from -1.5 to 1.5
- w_up: bfloat16 [768, 3072], P(None, 'tensor'), may hold values from -0.21875 to 0.21875
- b_up: float32 [3072], P('tensor'), may hold values from -1.5 to 1.5
- w_down: bfloat16 [3072, 768], P('tensor'), may hold values from -0.109375 to 0.109375
- b_down: float32 [768], replicated, may hold values from -1.5 to 1.5
Outputs:
- outputs: bfloat16 [16384, 768], P('dp')
- grad_inputs: float32 [16384, 768], P('dp')
- grad_first_values: float32 [16384, 384], P('dp')
- grad_pre_attn_gain: float32 [768], replicated
- grad_pre_attn_bias: float32 [768], replicated
- grad_w_query: float32 [768, 768], P(None, 'tensor')
- grad_w_key: float32 [768, 768], P(None, 'tensor')
- grad_w_value: float32 [768, 384], replicated
- grad_w_out: float32 [768, 768], P('tensor')
- grad_pre_mlp_gain: float32 [768], replicated
- grad_pre_mlp_bias: float32 [768], replicated
- grad_w_up: float32 [768, 3072], P(None, 'tensor')
- grad_b_up: float32 [3072], P('tensor')
- grad_w_down: float32 [3072, 768], P('tensor')
- grad_b_down: float32 [768], replicated
Inputs may be any that keep to these rules, and one draw needn't show every extreme that they name: `piece_start`: piece p of a sequence lies within tokens p * (512) to (p + 1) * 512 - 1. `piece_length`: the first piece of every sequence has 256 tokens.
All inputs are finite; a program needn't handle non-finite values.
Results may differ from a plain program's by a relative error of at most 0.017.
Values may be sent and summed in bfloat16 or wider, within the bound.
No kernel may reach another device: no remote copies, remote signals or barrier semaphores. Data moves between devices by JAX's collectives and lax.ppermute only.
A program may use at most 128 MiB of HBM per device.

v0:
```python
from functools import partial
import math

import jax
import jax.numpy as jnp
from jax import lax
from jax.sharding import PartitionSpec as P

HEADS = 12
HD = 64
VFRESH = 6


score_scale = 0.125
far_below = -1e30
epsilon = 1e-05


def transposed_times(left, right):
    return lax.dot_general(
        left, right, (((0,), (0,)), ((), ())), preferred_element_type=jnp.float32
    )


def times_transposed(left, right):
    return lax.dot_general(
        left, right, (((1,), (1,)), ((), ())), preferred_element_type=jnp.float32
    )


def normalize(values, norm_gain, norm_shift):
    centered = values - jnp.mean(values, axis=-1, keepdims=True)
    inverse = lax.rsqrt(jnp.mean(centered * centered, axis=-1, keepdims=True) + epsilon)
    normal_part = centered * inverse
    return (normal_part * norm_gain + norm_shift, normal_part, inverse)


def norm_backward(upstream, normal_part, inverse, norm_gain):
    scaled = upstream * norm_gain
    inner_term = (
        scaled
        - jnp.mean(scaled, axis=-1, keepdims=True)
        - normal_part * jnp.mean(scaled * normal_part, axis=-1, keepdims=True)
    )
    return (
        inverse * inner_term,
        jnp.sum(upstream * normal_part, axis=0),
        jnp.sum(upstream, axis=0),
    )


def piece_labels(starts, lengths, length):
    places = jnp.arange(length, dtype=jnp.int32)
    inside = (places[None, None, :] >= starts[:, :, None]) & (
        places[None, None, :] < (starts + lengths)[:, :, None]
    )
    numbers = jnp.arange(1, starts.shape[1] + 1, dtype=jnp.int32)
    return jnp.sum(jnp.where(inside, numbers[None, :, None], 0), axis=1)


def block_scores(queries, keys_low, labels, row_start, block_rows, local_heads):
    length = keys_low.shape[0]
    query_block = lax.dynamic_slice_in_dim(queries, row_start, block_rows, 0).reshape(
        block_rows, local_heads, -1
    )
    scores = (
        jnp.einsum(
            "qhe,khe->hqk",
            query_block,
            keys_low.reshape(length, local_heads, -1),
            preferred_element_type=jnp.float32,
        )
        * score_scale
    )
    query_pos = row_start + jnp.arange(block_rows, dtype=jnp.int32)
    key_pos = jnp.arange(length, dtype=jnp.int32)
    query_labels = lax.dynamic_slice_in_dim(labels, row_start, block_rows, 0)
    allowed = (key_pos[None, :] <= query_pos[:, None]) | (
        query_labels[:, None] == labels[None, :]
    ) & (query_labels[:, None] > 0)
    return (jnp.where(allowed[None], scores, far_below), query_block)


def attend_forward(operands, local_heads, block_rows):
    queries, keys_low, values, labels = operands
    length = queries.shape[0]
    values_heads = values.reshape(length, local_heads, -1)

    def one_block(block_index):
        scores, _ = block_scores(
            queries, keys_low, labels, block_index * block_rows, block_rows, local_heads
        )
        row_peak = jnp.max(scores, axis=-1, keepdims=True)
        raw_weights = jnp.exp(scores - row_peak)
        row_total = jnp.sum(raw_weights, axis=-1, keepdims=True)
        attn_probs = (raw_weights / row_total).astype(jnp.bfloat16)
        mixed_heads = jnp.einsum(
            "hqk,khe->qhe", attn_probs, values_heads, preferred_element_type=jnp.float32
        )
        return (
            mixed_heads.reshape(block_rows, -1).astype(jnp.bfloat16),
            (row_peak + jnp.log(row_total))[..., 0],
        )

    mixed_heads, log_sums = lax.map(one_block, jnp.arange(length // block_rows))
    return (
        mixed_heads.reshape(length, -1),
        jnp.transpose(log_sums, (1, 0, 2)).reshape(local_heads, length),
    )


def attend_backward(operands, local_heads, block_rows):
    queries, keys_low, values, labels, log_sums, grad_mixed = operands
    length = queries.shape[0]
    keys_heads = keys_low.reshape(length, local_heads, -1)
    values_heads = values.reshape(length, local_heads, -1)

    def one_block(running, block_index):
        grad_keys, grad_values = running
        row_start = block_index * block_rows
        scores, query_block = block_scores(
            queries, keys_low, labels, row_start, block_rows, local_heads
        )
        attn_probs = jnp.exp(
            scores - lax.dynamic_slice_in_dim(log_sums, row_start, block_rows, 1)[..., None]
        )
        grad_block = lax.dynamic_slice_in_dim(grad_mixed, row_start, block_rows, 0).reshape(
            block_rows, local_heads, -1
        )
        grad_probs = jnp.einsum(
            "qhe,khe->hqk", grad_block, values_heads, preferred_element_type=jnp.float32
        )
        grad_scores = (
            attn_probs * (grad_probs - jnp.sum(attn_probs * grad_probs, axis=-1, keepdims=True))
        ).astype(jnp.bfloat16)
        grad_query = (
            jnp.einsum("hqk,khe->qhe", grad_scores, keys_heads, preferred_element_type=jnp.float32)
            * score_scale
        )
        grad_keys = (
            grad_keys
            + jnp.einsum(
                "hqk,qhe->khe", grad_scores, query_block, preferred_element_type=jnp.float32
            )
            * score_scale
        )
        grad_values = grad_values + jnp.einsum(
            "hqk,qhe->khe",
            attn_probs.astype(jnp.bfloat16),
            grad_block,
            preferred_element_type=jnp.float32,
        )
        return ((grad_keys, grad_values), grad_query.reshape(block_rows, -1))

    start_sums = (
        jnp.zeros(keys_heads.shape, jnp.float32),
        jnp.zeros(values_heads.shape, jnp.float32),
    )
    (grad_keys, grad_values), grad_queries = lax.scan(
        one_block, start_sums, jnp.arange(length // block_rows)
    )
    return (
        grad_queries.reshape(length, -1),
        grad_keys.reshape(length, -1),
        grad_values.reshape(length, -1),
    )


def on_device(
    inputs,
    first_values,
    piece_start,
    piece_length,
    cotangent,
    pre_attn_gain,
    pre_attn_bias,
    w_query,
    w_key,
    w_value,
    w_out,
    pre_mlp_gain,
    pre_mlp_bias,
    w_up,
    b_up,
    w_down,
    b_down,
):
    groups = lax.axis_size("tensor")
    member = lax.axis_index("tensor")
    local_heads = HEADS // groups
    columns = local_heads * HD
    is_fresh = member < VFRESH // local_heads
    tokens_dev, width = inputs.shape
    value_width = w_value.shape[1]
    seq_count = piece_start.shape[0]
    length = tokens_dev // seq_count
    block_rows = math.gcd(512, length)
    labels = piece_labels(piece_start, piece_length, length)

    def by_sequence(matrix):
        return matrix.reshape(seq_count, length, -1)

    x_float = inputs.astype(jnp.float32)
    attn_in, attn_normal, attn_inverse = normalize(x_float, pre_attn_gain, pre_attn_bias)
    attn_low = attn_in.astype(jnp.bfloat16)
    queries = jnp.dot(attn_low, w_query, preferred_element_type=jnp.float32).astype(jnp.bfloat16)
    keys_low = jnp.dot(attn_low, w_key, preferred_element_type=jnp.float32).astype(jnp.bfloat16)
    value_cols = lax.dynamic_slice_in_dim(
        w_value, jnp.minimum(member * columns, value_width - columns), columns, 1
    )
    first_cols = lax.dynamic_slice_in_dim(
        first_values, jnp.maximum(member * columns - value_width, 0), columns, 1
    )
    values = lax.cond(
        is_fresh,
        lambda: jnp.dot(attn_low, value_cols, preferred_element_type=jnp.float32).astype(
            jnp.bfloat16
        ),
        lambda: first_cols,
    )
    mixed_heads, log_sums = lax.map(
        partial(attend_forward, local_heads=local_heads, block_rows=block_rows),
        (by_sequence(queries), by_sequence(keys_low), by_sequence(values), labels),
    )
    mixed_heads = mixed_heads.reshape(tokens_dev, columns)
    attn_out = lax.psum(
        jnp.dot(mixed_heads, w_out, preferred_element_type=jnp.float32).astype(jnp.bfloat16),
        "tensor",
    ).astype(jnp.float32)
    hidden = x_float + attn_out
    mlp_in, mlp_normal, mlp_inverse = normalize(hidden, pre_mlp_gain, pre_mlp_bias)
    mlp_low = mlp_in.astype(jnp.bfloat16)
    pre_act = jnp.dot(mlp_low, w_up, preferred_element_type=jnp.float32) + b_up
    active = jax.nn.gelu(pre_act, approximate=True).astype(jnp.bfloat16)
    mlp_out = lax.psum(
        jnp.dot(active, w_down, preferred_element_type=jnp.float32).astype(jnp.bfloat16), "tensor"
    ).astype(jnp.float32)
    outputs = (hidden + mlp_out + b_down).astype(jnp.bfloat16)
    grad_out = cotangent.astype(jnp.float32)
    grad_b_down = jnp.sum(grad_out, axis=0)
    grad_w_down = transposed_times(active, cotangent)
    grad_active = times_transposed(cotangent, w_down)
    _, gelu_pull = jax.vjp(partial(jax.nn.gelu, approximate=True), pre_act)
    grad_pre = gelu_pull(grad_active)[0].astype(jnp.bfloat16)
    grad_b_up = jnp.sum(grad_pre.astype(jnp.float32), axis=0)
    grad_w_up = transposed_times(mlp_low, grad_pre)
    grad_mlp_in = lax.psum(times_transposed(grad_pre, w_up).astype(jnp.bfloat16), "tensor").astype(
        jnp.float32
    )
    grad_from_mlp, grad_mlp_gain, grad_mlp_bias = norm_backward(
        grad_mlp_in, mlp_normal, mlp_inverse, pre_mlp_gain
    )
    grad_hidden = grad_out + grad_from_mlp
    grad_hidden_low = grad_hidden.astype(jnp.bfloat16)
    grad_w_out = transposed_times(mixed_heads, grad_hidden_low)
    grad_mixed = times_transposed(grad_hidden_low, w_out).astype(jnp.bfloat16)
    grad_queries, grad_keys, grad_values = lax.map(
        partial(attend_backward, local_heads=local_heads, block_rows=block_rows),
        (
            by_sequence(queries),
            by_sequence(keys_low),
            by_sequence(values),
            labels,
            log_sums,
            by_sequence(grad_mixed),
        ),
    )
    query_grad_low = grad_queries.reshape(tokens_dev, columns).astype(jnp.bfloat16)
    key_grad_low = grad_keys.reshape(tokens_dev, columns).astype(jnp.bfloat16)
    grad_values = grad_values.reshape(tokens_dev, columns)
    value_grad_low = grad_values.astype(jnp.bfloat16)
    grad_w_query = transposed_times(attn_low, query_grad_low)
    grad_w_key = transposed_times(attn_low, key_grad_low)
    value_part = lax.cond(
        is_fresh,
        lambda: times_transposed(value_grad_low, value_cols),
        lambda: jnp.zeros((tokens_dev, width), jnp.float32),
    )
    grad_attn_in = lax.psum(
        (
            times_transposed(query_grad_low, w_query)
            + times_transposed(key_grad_low, w_key)
            + value_part
        ).astype(jnp.bfloat16),
        "tensor",
    ).astype(jnp.float32)
    grad_value_cols = lax.cond(
        is_fresh,
        lambda: transposed_times(attn_low, value_grad_low),
        lambda: jnp.zeros((width, columns), jnp.float32),
    )
    grad_first_cols = jnp.where(is_fresh, jnp.zeros_like(grad_values), grad_values)
    gathered_value, gathered_first = (
        lax.all_gather(grad_value_cols.astype(jnp.bfloat16), "tensor", axis=1, tiled=True).astype(
            grad_value_cols.dtype
        ),
        lax.all_gather(grad_first_cols.astype(jnp.bfloat16), "tensor", axis=1, tiled=True).astype(
            grad_first_cols.dtype
        ),
    )
    grad_w_value = gathered_value[:, :value_width]
    grad_first_values = gathered_first[:, value_width:]
    grad_from_attn, grad_attn_gain, grad_attn_bias = norm_backward(
        grad_attn_in, attn_normal, attn_inverse, pre_attn_gain
    )
    grad_inputs = grad_hidden + grad_from_attn
    all_sums = lax.psum(
        (
            grad_attn_gain,
            grad_attn_bias,
            grad_w_query,
            grad_w_key,
            grad_w_value,
            grad_w_out,
            grad_mlp_gain,
            grad_mlp_bias,
            grad_w_up,
            grad_b_up,
            grad_w_down,
            grad_b_down,
        ),
        "dp",
    )
    (
        grad_attn_gain,
        grad_attn_bias,
        grad_w_query,
        grad_w_key,
        grad_w_value,
        grad_w_out,
        grad_mlp_gain,
        grad_mlp_bias,
        grad_w_up,
        grad_b_up,
        grad_w_down,
        grad_b_down,
    ) = all_sums
    return (
        outputs,
        grad_inputs,
        grad_first_values,
        grad_attn_gain,
        grad_attn_bias,
        grad_w_query,
        grad_w_key,
        grad_w_value,
        grad_w_out,
        grad_mlp_gain,
        grad_mlp_bias,
        grad_w_up,
        grad_b_up,
        grad_w_down,
        grad_b_down,
    )


def solution(mesh):
    return jax.shard_map(
        on_device,
        mesh=mesh,
        in_specs=(
            P("dp", None),
            P("dp", None),
            P("dp", None),
            P("dp", None),
            P("dp", None),
            P(),
            P(),
            P(None, "tensor"),
            P(None, "tensor"),
            P(),
            P("tensor", None),
            P(),
            P(),
            P(None, "tensor"),
            P("tensor"),
            P("tensor", None),
            P(),
        ),
        out_specs=(
            P("dp", None),
            P("dp", None),
            P("dp", None),
            P(),
            P(),
            P(None, "tensor"),
            P(None, "tensor"),
            P(),
            P("tensor", None),
            P(),
            P(),
            P(None, "tensor"),
            P("tensor"),
            P("tensor", None),
            P(),
        ),
        check_vma=False,
    )
```

profile of v0, /device:TPU:0, one launch (start us, length us, event | category | flops | bytes accessed | tf_op | source)
XLA Modules:
  0.0 799.5 jit_solution(14310352117921144776)
XLA Ops:
  7.3 2.5 convert_reduce_fusion.2
  9.8 2.9 fusion.37
  13.1 4.0 fusion.33
  17.1 3.1 convolution_convert_fusion.6
  20.2 3.1 convolution_convert_fusion.5
  24.7 4.8 conditional.3
  24.7 3.1 convolution_convert_fusion
  29.5 36.7 %while.60 = (s32[]{:T(128)}, bf16[2,1024,192]{2,1,0:T(8,128)(2,1)}, f32[2,3,1024]{2,1,0:T(4,128)S(1)}, bf16[2,1024,192]{1,2,0:T(8,128)(2,1)}, bf16[2,1024,192]{1...) while((s32[]{:T(128)}, bf16[2,1024,192]{2,1,0:T(8,128)(2,1)}, ...), condition=%wide.region_10.11_spmd.clone, body=%wide.region_5.10_spmd.sunk.clone | while | flops 423722496 | bytes 27113392 | solution.py:221
  31.8 15.0 %while.59 = (s32[]{:T(128)}, bf16[2,512,192]{1,2,0:T(8,128)(2,1)S(1)}, f32[2,3,512]{2,1,0:T(4,128)S(1)}, s32[2]{0:T(128)S(1)}, s32[1024]{0:T(1024)S(1)}, /*index...) while((s32[]{:T(128)}, ...), condition=%wide.region_9.9_spmd, body=%wide.region_6.8_spmd.sunk | while | flops 423722496 | bytes 23008452 | solution.py:105
  50.1 15.0 %while.59 = (s32[]{:T(128)}, bf16[2,512,192]{1,2,0:T(8,128)(2,1)S(1)}, f32[2,3,512]{2,1,0:T(4,128)S(1)}, s32[2]{0:T(128)S(1)}, s32[1024]{0:T(1024)S(1)}, /*index...) while((s32[]{:T(128)}, ...), condition=%wide.region_9.9_spmd, body=%wide.region_6.8_spmd.sunk | while | flops 423722496 | bytes 23008452 | solution.py:105
  55.4 2.2 fusion.152
  62.9 2.2 fusion.152
  66.2 3.9 convolution_convert_fusion.3
  70.7 69.8 %all-reduce.8.cloned.1.call-done = bf16[2048,768]{1,0:T(8,128)(2,1)} async-done(((bf16[2048,768]{1,0:T(8,128)(2,1)}), bf16[2048,768]{1,0:T(8,128)(2,1)}) %all-reduce.8.cloned.1.call-update) | async-done | bytes 3145744 | tf_op jit(solution)/shard_map/psum | solution.py:226
  140.5 3.9 fusion.51
  146.8 3.6 fusion.56
  150.5 8.3 %convert_reduce_fusion.4 = (f32[768]{0:T(1024)}, bf16[2048,768]{1,0:T(8,128)(2,1)S(1)}, bf16[2048,768]{1,0:T(8,128)(2,1)}) fusion(f32[2048,768]{1,0:T(8,128)S(1)} %fusion.56, f32[768]{0:T(1024)S(1)} %copy-done.51, bf16[2048,768]{1,0:T(8,128)(2,1)S(1)} %copy-done.19, bf16[768,768]{1,0:T(8,128)(2,1)S(1)} %copy-done), kind=kOutput, calls=%fused_computation.97 | convolution fusion | flops 2455239936 | bytes 16914432 | tf_op jit(solution)/shard_map/dot_general | solution.py:26
  160.4 4.0 convolution_convert_fusion.1
  164.7 68.4 %all-reduce.10.cloned.1.call-done = bf16[2048,768]{1,0:T(8,128)(2,1)} async-done(((bf16[2048,768]{1,0:T(8,128)(2,1)}), bf16[2048,768]{1,0:T(8,128)(2,1)}) %all-reduce.10.cloned.1.call-update) | async-done | bytes 3145744 | tf_op jit(solution)/shard_map/psum | solution.py:247
  233.2 7.7 fusion.49
  240.9 5.7 convert_reduce_fusion.3
  246.6 2.7 copy-done.7
  251.4 96.6 %while.62 = (s32[]{:T(128)}, bf16[2,1024,192]{2,1,0:T(8,128)(2,1)}, bf16[2,1024,192]{1,2,0:T(8,128)(2,1)}, bf16[2,1024,192]{1,2,0:T(8,128)(2,1)}, bf16[2,1024,19...) while((s32[]{:T(128)}, bf16[2,1024,192]{2,1,0:T(8,128)(2,1)}, ...), condition=%wide.region_22.23_spmd.clone, body=%wide.region_18.22_spmd.sunk.clone | while | flops 1033502208 | bytes 118910104 | solution.py:257
  255.4 39.5 %while.61 = (s32[]{:T(128)}, f32[1024,3,64]{0,2,1:T(8,128)S(1)}, f32[1024,3,64]{0,2,1:T(8,128)}, bf16[2,512,192]{1,2,0:T(8,128)(2,1)}, s32[2]{0:T(128)S(1)}, /*i...) while((s32[]{:T(128)}, f32[1024,3,64]{0,2,1:T(8,128)S(1)}, ...), condition=%wide.region_21.21_spmd.clone, body=%wide.region_19.20_spmd.clone.sunk | while | flops 1033502208 | bytes 110880112 | solution.py:159
  259.6 2.5 multiply_reduce_fusion.3
  262.2 2.9 multiply_convert_fusion.3
  265.1 2.8 fusion.144
  267.9 3.0 convolution_multiply_fusion.3
  271.7 2.9 fusion.145
  278.8 2.5 multiply_reduce_fusion.3
  281.4 2.9 multiply_convert_fusion.3
  284.3 2.8 fusion.144
  287.1 3.0 convolution_multiply_fusion.3
  290.9 4.0 fusion.145
  303.8 39.5 %while.61 = (s32[]{:T(128)}, f32[1024,3,64]{0,2,1:T(8,128)S(1)}, f32[1024,3,64]{0,2,1:T(8,128)}, bf16[2,512,192]{1,2,0:T(8,128)(2,1)}, s32[2]{0:T(128)S(1)}, /*i...) while((s32[]{:T(128)}, f32[1024,3,64]{0,2,1:T(8,128)S(1)}, ...), condition=%wide.region_21.21_spmd.clone, body=%wide.region_19.20_spmd.clone.sunk | while | flops 1033502208 | bytes 110880112 | solution.py:159
  307.9 2.5 multiply_reduce_fusion.3
  310.5 2.9 multiply_convert_fusion.3
  313.5 2.8 fusion.144
  316.2 3.0 convolution_multiply_fusion.3
  320.1 2.9 fusion.145
  327.1 2.5 multiply_reduce_fusion.3
  329.7 2.9 multiply_convert_fusion.3
  332.6 2.8 fusion.144
  335.4 3.0 convolution_multiply_fusion.3
  339.2 4.0 fusion.145
  349.7 2.7 conditional.5
  349.7 2.7 fusion.61
  353.3 6.2 convolution_convert_fusion.2
  359.6 3.7 conditional.4
  359.6 3.7 fusion.60
  366.6 2.9 add_convert_fusion
  372.1 7.1 fusion.65
  379.3 4.6 fusion.55
  383.9 3.6 fusion.66
  387.5 3.5 fusion.64
  395.0 97.7 %all-reduce.14.cloned.1.call-done = (bf16[2048,768]{1,0:T(8,128)(2,1)}, bf16[2048,768]{1,0:T(8,128)(2,1)}) async-done(((bf16[2048,768]{1,0:T(8,128)(2,1)}, bf16[2048,768]{1,0:T(8,128)(2,1)}), (bf16[2048,768]{1,0:T(8,128)(2,1)}, bf16[2048,768]{1,0:T(8,128)(2,1)})) %all-reduce.14.cloned.1.call-update) | async-done | bytes 6291472 | tf_op jit(solution)/shard_map/psum | solution.py:235
  492.7 5.0 fusion.50
  497.8 38.2 %all-reduce = (f32[768]{0:T(1024)}, f32[768]{0:T(1024)}, f32[768]{0:T(1024)}, f32[768]{0:T(1024)}, f32[768]{0:T(1024)}, /*index=5*/f32[768]{0:T(1024)}) all-reduce(f32[768]{0:T(1024)S(1)} %get-tuple-element.409, f32[768]{0:T(1024)S(1)} %get-tuple-element.414, f32[768]{0:T(1024)S(1)} %copy-done.42, ...), channel_id=1, replica_groups=mesh['dp'=8,'tensor'=4] {'dp'}, use_global_device_ids=true, to_apply=%region_29.30 | all-reduce | flops 4608 | bytes 36864 | tf_op jit(solution)/shard_map/psum | solution.py:307
  535.9 11.9 %fusion.36 = (f32[2048,768]{1,0:T(8,128)}, bf16[2048,768]{1,0:T(8,128)(2,1)}) fusion(f32[2048,768]{1,0:T(8,128)} %copy-done.7, bf16[2048,768]{1,0:T(8,128)(2,1)} %param.31, bf16[2048,768]{1,0:T(8,128)(2,1)} %get-tuple-element.502, f32[2048]{0:T(1024)S(1)} %broadcast_multiply_fusion, f32[2048]{0:T(1024)S(1)} %broadcast_multiply_fusion.1, ...), kind=kLoop, calls=%fused_computation.82 | loop fusion | flops 25165824 | bytes 28350464 | tf_op jit(solution)/shard_map/add | solution.py:306
  547.9 3.5 slice_convert_fusion
  551.4 3.5 copy.92
  554.9 224.1 %all-reduce.12.cloned.1.call-done = (f32[768,192]{0,1:T(8,128)}, f32[768,192]{0,1:T(8,128)}, f32[768,384]{0,1:T(8,128)}, f32[192,768]{1,0:T(8,128)}, f32[768,768]{1,0:T(8,128)}, /*index=5*/f32[768,768]{1,0:T(8,128)}) async-done(((f32[768,192]{0,1:T(8,128)}, f32[768,192]{0,1:T(8,128)}, f32[768,384]{0,1:T(8,128)}, f32[192,768]{1,0:T(8,128)}, f32[768,768]{1,0:T(8,128)}, /*index=5*/f32[768,768]{1,0:T(8,128)}), ...) | async-done | bytes 7667728 | tf_op jit(solution)/shard_map/psum | solution.py:307
  779.0 2.8 copy.93
  787.6 3.2 copy.199
  (306 shorter events, 94.1 us)
Async XLA Ops:
  7.2 143.3 %copy-start = (bf16[768,768]{1,0:T(8,128)(2,1)S(1)}, bf16[768,768]{1,0:T(8,128)(2,1)}, u32[]{:S(2)}) copy-start(bf16[768,768]{1,0:T(8,128)(2,1)} %param.46) | copy-start | bytes 3538948
  7.2 5.6 copy-start.29
  7.2 5.8 copy-start.38
  7.2 5.8 copy-start.45
  7.2 133.3 %all-reduce.8.cloned.1.call-start = ((), (), s32[]{:S(2)}) async-start(), calls=%async_computation | async-start | bytes 6291456 | tf_op jit(solution)/shard_map/psum | solution.py:226
  7.3 9.7 %copy-start.27 = (bf16[768,192]{0,1:T(8,128)(2,1)S(1)}, bf16[768,192]{0,1:T(8,128)(2,1)}, u32[]{:S(2)}) copy-start(bf16[768,192]{0,1:T(8,128)(2,1)} %param.38) | copy-start | bytes 884740
  9.8 10.3 %copy-start.30 = (f32[2048]{0:T(1024)}, f32[2048]{0:T(1024)S(1)}, u32[]{:S(2)}) copy-start(f32[2048]{0:T(1024)S(1)} %broadcast_multiply_fusion.5) | copy-start | bytes 24580
  12.8 7.3 copy-start.32
  13.0 11.6 %copy-start.16 = (bf16[768,192]{1,0:T(8,128)(2,1)}, bf16[768,192]{1,0:T(8,128)(2,1)S(1)}, u32[]{:S(2)}) copy-start(bf16[768,192]{1,0:T(8,128)(2,1)S(1)} %constant_dynamic-slice_fusion.10) | copy-start | bytes 884740
  13.1 7.1 copy-start.26
  20.1 4.4 copy-start.48
  20.2 4.4 copy-start.49
  29.5 36.7 %copy-start.21 = (bf16[192,768]{1,0:T(8,128)(2,1)S(1)}, bf16[192,768]{1,0:T(8,128)(2,1)}, u32[]{:S(2)}) copy-start(bf16[192,768]{1,0:T(8,128)(2,1)} %param.41) | copy-start | bytes 884740
  70.1 76.7 %copy-start.50 = (bf16[768,768]{1,0:T(8,128)(2,1)S(1)}, bf16[768,768]{1,0:T(8,128)(2,1)}, u32[]{:S(2)}) copy-start(bf16[768,768]{1,0:T(8,128)(2,1)} %param.44) | copy-start | bytes 3538948
  70.1 76.7 %copy-start.40 = (f32[768]{0:T(1024)S(1)}, f32[768]{0:T(1024)}, u32[]{:S(2)}) copy-start(f32[768]{0:T(1024)} %param.42) | copy-start | bytes 9220
  70.1 76.7 %copy-start.52 = (f32[768]{0:T(1024)S(1)}, f32[768]{0:T(1024)}, u32[]{:S(2)}) copy-start(f32[768]{0:T(1024)} %param.43) | copy-start | bytes 9220
  70.1 163.0 %all-reduce.10.cloned.1.call-start = ((), (), s32[]{:S(2)}) async-start(), calls=%async_computation.1 | async-start | bytes 6291456 | tf_op jit(solution)/shard_map/psum | solution.py:247
  140.5 3.9 copy-start.4
  140.5 4.7 copy-start.8
  145.2 95.7 %copy-start.34 = (f32[2048]{0:T(1024)}, f32[2048]{0:T(1024)S(1)}, u32[]{:S(2)}) copy-start(f32[2048]{0:T(1024)S(1)} %broadcast_multiply_fusion.4) | copy-start | bytes 24580
  146.8 94.1 %copy-start.36 = (f32[2048]{0:T(1024)}, f32[2048]{0:T(1024)S(1)}, u32[]{:S(2)}) copy-start(f32[2048]{0:T(1024)S(1)} %add_rsqrt_fusion) | copy-start | bytes 24580
  146.8 3.6 copy-start.19
  146.8 3.6 copy-start.51
  164.5 228.3 %all-gather.5.cloned.1.call-start = ((), (), s32[]{:S(2)}) async-start(), calls=%async_computation.3 | async-start | bytes 1474560 | tf_op jit(solution)/shard_map/all_gather | solution.py:294
  233.2 7.7 copy-start.5
  233.2 7.8 copy-start.9
  233.2 7.8 copy-start.12
  256.7 2.9 copy-start.3
  265.1 5.8 copy-start.13
  265.1 6.6 copy-start.2
  275.9 2.9 copy-start.3
  284.3 5.8 copy-start.13
  284.3 6.6 copy-start.2
  313.5 5.8 copy-start.13
  313.5 6.6 copy-start.2
  324.2 2.9 copy-start.3
  332.6 5.8 copy-start.13
  332.6 6.6 copy-start.2
  353.2 139.5 %all-reduce.14.cloned.1.call-start = ((), (), s32[]{:S(2)}) async-start(), calls=%async_computation.5 | async-start | bytes 12582912 | tf_op jit(solution)/shard_map/psum | solution.py:235
  353.2 6.3 copy-start.17
  353.2 6.2 copy-start.25
  363.3 3.3 copy-start.11
  369.5 178.4 %all-gather.3.cloned.1.call-start = ((), (), s32[]{:S(2)}) async-start(), calls=%async_computation.2 | async-start | bytes 3932160 | tf_op jit(solution)/shard_map/all_gather | solution.py:297
  371.7 7.5 copy-start.35
  371.8 7.4 copy-start.37
  371.8 7.4 copy-start.41
  371.8 7.4 copy-start.53
  371.8 407.2 %all-reduce.12.cloned.1.call-start = ((), (), s32[]{:S(2)}) async-start(), calls=%async_computation.4 | async-start | bytes 15335424 | tf_op jit(solution)/shard_map/psum | solution.py:307
  372.1 7.1 copy-start.6
  372.1 7.1 copy-start.10
  372.1 7.1 copy-start.55
  372.1 18.9 %slice-start = ((s8[6291456]{0:T(1024)(128)(4,1)}), s8[4194304]{0:T(1024)(128)(4,1)S(1)}, s32[]{:S(2)}) async-start(s8[6291456]{0:T(1024)(128)(4,1)} %bitcast.223), calls=%async_computation.6 | async-start | bytes 8388608
  379.2 8.2 %copy-start.24 = (bf16[2,1024,192]{2,1,0:T(8,128)(2,1)S(1)}, bf16[2,1024,192]{2,1,0:T(8,128)(2,1)}, u32[]{:S(2)}) copy-start(bf16[2,1024,192]{2,1,0:T(8,128)(2,1)} %get-tuple-element.264) | copy-start | bytes 2359300
  379.3 11.7 %slice-start.1 = ((s8[6291456]{0:T(1024)(128)(4,1)}), s8[2097152]{0:T(1024)(128)(4,1)S(1)}, s32[]{:S(2)}) async-start(s8[6291456]{0:T(1024)(128)(4,1)} %bitcast.223), calls=%async_computation.7 | async-start | bytes 4194304
  383.9 7.1 copy-start.15
  392.7 100.0 %copy-start.31 = (f32[2048]{0:T(1024)S(1)}, f32[2048]{0:T(1024)}, u32[]{:S(2)}) copy-start(f32[2048]{0:T(1024)} %copy-done.30) | copy-start | bytes 24580
  392.7 100.0 %copy-start.33 = (f32[2048]{0:T(1024)S(1)}, f32[2048]{0:T(1024)}, u32[]{:S(2)}) copy-start(f32[2048]{0:T(1024)} %copy-done.32) | copy-start | bytes 24580
  392.7 100.0 %copy-start.39 = (f32[768]{0:T(1024)S(1)}, f32[768]{0:T(1024)}, u32[]{:S(2)}) copy-start(f32[768]{0:T(1024)} %param.36) | copy-start | bytes 9220
  394.9 102.8 %copy-start.42 = (f32[768]{0:T(1024)S(1)}, f32[768]{0:T(1024)}, u32[]{:S(2)}) copy-start(f32[768]{0:T(1024)} %get-tuple-element.407) | copy-start | bytes 9220
  394.9 102.8 %copy-start.43 = (f32[768]{0:T(1024)S(1)}, f32[768]{0:T(1024)}, u32[]{:S(2)}) copy-start(f32[768]{0:T(1024)} %get-tuple-element.413) | copy-start | bytes 9220
  394.9 102.8 %copy-start.44 = (f32[768]{0:T(1024)S(1)}, f32[768]{0:T(1024)}, u32[]{:S(2)}) copy-start(f32[768]{0:T(1024)} %get-tuple-element.522) | copy-start | bytes 9220
  394.9 102.8 %copy-start.47 = (f32[768]{0:T(1024)S(1)}, f32[768]{0:T(1024)}, u32[]{:S(2)}) copy-start(f32[768]{0:T(1024)} %get-tuple-element.507) | copy-start | bytes 9220
  394.9 141.0 %copy-start.46 = (f32[768]{0:T(1024)S(1)}, f32[768]{0:T(1024)}, u32[]{:S(2)}) copy-start(f32[768]{0:T(1024)} %param.47) | copy-start | bytes 9220
  779.0 11.8 %copy-start.20 = (f32[768,768]{1,0:T(8,128)S(1)}, f32[768,768]{1,0:T(8,128)}, u32[]{:S(2)}) copy-start(f32[768,768]{1,0:T(8,128)} %get-tuple-element.1089) | copy-start | bytes 7077892
  (15 other events, 27.0 us)
Sparse Core Ops, SparseCore 0:
  70.2 70.2 all-reduce.7
  164.6 68.5 all-reduce.9
  353.3 17.4 all-gather.4
  373.0 119.6 all-reduce.13
  494.1 28.7 all-gather.2
  529.1 249.8 all-reduce.11
where the time goes:
time: 809 us; the launch traced here: 800 us
  waiting for transfers between devices  460 us (57%)
  matrix products  134 us (17%)
  other arithmetic  76.1 us (9%)
  local copies, waits for them, and re-layouts  68.7 us (8%)
  blocking collectives  38.2 us (5%)
  between operations  15.3 us (2%)
    psum x1, waiting for transfers between devices, on_device(): lax.psum((grad_attn_gain, grad_attn_bias, grad_w_query, grad_w_key, grad_...  224 us
    psum x1, waiting for transfers between devices, on_device(): lax.psum(jnp.dot(active, w_down, preferred_element_type=jnp.float32).asty...  97.7 us
    psum x1, waiting for transfers between devices, on_device(): lax.psum(jnp.dot(mixed_heads, w_out, preferred_element_type=jnp.float32)....  69.8 us
    psum x1, waiting for transfers between devices, on_device(): lax.psum(times_transposed(grad_pre, w_up).astype(jnp.bfloat16), 'tensor')  68.4 us
    psum x1, blocking collectives, on_device(): lax.psum((grad_attn_gain, grad_attn_bias, grad_w_query, grad_w_key, grad_...  38.2 us
    unnamed x113, local copies, waits for them, and re-layouts  25.1 us
    dot_general x6, matrix products, transposed_times(): lax.dot_general(left, right, (((0,), (0,)), ((), ())), preferred_element_...  23.2 us
    dot_general x6, matrix products, times_transposed(): lax.dot_general(left, right, (((1,), (1,)), ((), ())), preferred_element_...  22.2 us
  transfers between devices with their start and end apart: 6, of which 4 were waited for; matrix products, arithmetic and copies ran while one was open for 8% of the time, Pallas kernels for 0%

commit v1 on v0

v1 whole, which is shorter than its diff:
```python
from functools import partial

import jax
import jax.numpy as jnp
from jax import lax
from jax.experimental import pallas as pl
from jax.experimental.pallas import tpu as pltpu
from jax.sharding import PartitionSpec as P

HEADS = 12
HD = 64
VFRESH = 6

score_scale = 0.125
far_below = -1e30
epsilon = 1e-05

F32 = jnp.float32
BF16 = jnp.bfloat16
VMEM_BYTES = 56 << 20


def nn(left, right):
    return lax.dot_general(left, right, (((1,), (0,)), ((), ())), preferred_element_type=F32)


def nt(left, right):
    return lax.dot_general(left, right, (((1,), (1,)), ((), ())), preferred_element_type=F32)


def tn(left, right):
    return lax.dot_general(left, right, (((0,), (0,)), ((), ())), preferred_element_type=F32)


def normal_parts(values):
    centered = values - jnp.mean(values, axis=-1, keepdims=True)
    inverse = lax.rsqrt(jnp.mean(centered * centered, axis=-1, keepdims=True) + epsilon)
    return centered * inverse, inverse


def norm_pull(upstream, normal_part, inverse, norm_gain):
    scaled = upstream * norm_gain
    return inverse * (
        scaled
        - jnp.mean(scaled, axis=-1, keepdims=True)
        - normal_part * jnp.mean(scaled * normal_part, axis=-1, keepdims=True)
    )


def whole(shape):
    return pl.BlockSpec(shape, lambda *_: (0,) * len(shape))


def shaped(shape, dtype):
    return jax.ShapeDtypeStruct(shape, dtype)


def params(**more):
    return pltpu.CompilerParams(vmem_limit_bytes=VMEM_BYTES, **more)


def project_body(fresh, x_ref, gain_ref, shift_ref, wq_ref, wk_ref, wv_ref, first_ref, low_ref, q_ref, k_ref, v_ref):
    normal, _ = normal_parts(x_ref[...].astype(F32))
    low = (normal * gain_ref[...] + shift_ref[...]).astype(BF16)
    low_ref[...] = low
    q_ref[...] = nn(low, wq_ref[...]).astype(BF16)
    k_ref[...] = nn(low, wk_ref[...]).astype(BF16)

    @pl.when(fresh[0] == 1)
    def _():
        v_ref[...] = nn(low, wv_ref[...]).astype(BF16)

    @pl.when(fresh[0] == 0)
    def _():
        v_ref[...] = first_ref[...]


def project(fresh, x, gain, shift, wq, wk, wv, first, seq, length, rows=256):
    width, cols = wq.shape
    steps = length // rows
    at = lambda i, *_: (seq * steps + i, 0)
    out = lambda i, *_: (i, 0)
    return pl.pallas_call(
        project_body,
        out_shape=(shaped((length, width), BF16),) + (shaped((length, cols), BF16),) * 3,
        grid_spec=pltpu.PrefetchScalarGridSpec(
            num_scalar_prefetch=1,
            grid=(steps,),
            in_specs=[
                pl.BlockSpec((rows, width), at),
                whole((1, width)),
                whole((1, width)),
                whole((width, cols)),
                whole((width, cols)),
                whole((width, cols)),
                pl.BlockSpec((rows, cols), at),
            ],
            out_specs=(pl.BlockSpec((rows, width), out),) + (pl.BlockSpec((rows, cols), out),) * 3,
        ),
        compiler_params=params(),
        name="project",
    )(fresh, x, gain, shift, wq, wk, wv, first)


def span_bias(start, size, base, keys, rows, row0):
    key_pos = base + lax.broadcasted_iota(jnp.int32, (keys, rows), 0)
    query_pos = base + row0 + lax.broadcasted_iota(jnp.int32, (keys, rows), 1)
    stop = start + size
    both = (key_pos >= start) & (key_pos < stop) & (query_pos >= start) & (query_pos < stop)
    return jnp.where((key_pos <= query_pos) | both, 0.0, far_below)


def in_tile(part, head, width):
    if width == HD:
        return part
    zero = jnp.zeros_like(part)
    return jnp.concatenate([part, zero] if head % 2 == 0 else [zero, part], 0)


def store_half(side, half, rows, value, own_ref, other_ref):
    @pl.when(side == half)
    def _():
        own_ref[rows, :] = value

    @pl.when(side != half)
    def _():
        other_ref[rows, :] = value


def attend_body(
    side, start, size, q_ref, k_ref, v_ref, wo_ref, zt_ref, lse_ref, own_ref, other_ref, bias_ref, *, heads, span, rb, seq
):
    length = q_ref.shape[0]
    lanes = heads * HD
    half = length // 2
    vt = v_ref[...].T
    qt = (q_ref[...] * score_scale).T
    for p in range(length // span):
        for r in range(0, span, rb):
            bias_ref[:, r : r + rb] = span_bias(start[seq, p], size[seq, p], p * span, span, rb, r)
        before = p * span
        keys = before + span
        for r in range(0, span, rb):
            row0 = before + r
            outs = []
            for h in range(heads):
                lo = h // 2 * 2 * HD
                hi = min(lo + 2 * HD, lanes)
                qh = in_tile(qt[h * HD : (h + 1) * HD, row0 : row0 + rb], h, hi - lo)
                vth = vt[h * HD : (h + 1) * HD, :]
                scores = nn(k_ref[:keys, lo:hi], qh)
                diag = scores[before:] + bias_ref[:, r : r + rb]
                peak = jnp.max(diag, axis=0, keepdims=True)
                if p:
                    peak = jnp.maximum(peak, jnp.max(scores[:before], axis=0, keepdims=True))
                raw = jnp.exp(diag - peak)
                total = jnp.sum(raw, axis=0, keepdims=True)
                zt = nn(vth[:, before:keys], raw.astype(BF16))
                if p:
                    raw = jnp.exp(scores[:before] - peak)
                    total = total + jnp.sum(raw, axis=0, keepdims=True)
                    zt = zt + nn(vth[:, :before], raw.astype(BF16))
                outs.append((zt / total).astype(BF16))
                lse_ref[h : h + 1, row0 : row0 + rb] = peak + jnp.log(total)
            zt = jnp.concatenate(outs, 0)
            zt_ref[:, row0 : row0 + rb] = zt
            out = nn(zt.T, wo_ref[...]).astype(BF16)
            at = row0 % half
            store_half(side[0], row0 // half, slice(at, at + rb), out, own_ref, other_ref)


def attend(side, start, size, q, k, v, wo, heads, seq, rb=512):
    length, lanes = q.shape
    width = wo.shape[1]
    span = length // start.shape[1]
    rb = min(rb, span, length // 2)
    return pl.pallas_call(
        partial(attend_body, heads=heads, span=span, rb=rb, seq=seq),
        out_shape=(
            shaped((lanes, length), BF16),
            shaped((heads, length), F32),
            shaped((length // 2, width), BF16),
            shaped((length // 2, width), BF16),
        ),
        grid_spec=pltpu.PrefetchScalarGridSpec(
            num_scalar_prefetch=3,
            grid=(1,),
            in_specs=[whole(q.shape), whole(q.shape), whole(q.shape), whole(wo.shape)],
            out_specs=(
                whole((lanes, length)),
                whole((heads, length)),
                whole((length // 2, width)),
                whole((length // 2, width)),
            ),
            scratch_shapes=[pltpu.VMEM((span, span), F32)],
        ),
        compiler_params=params(),
        name="attend",
    )(side, start, size, q, k, v, wo)


def attend_pull_body(
    side, start, size, q_ref, k_ref, v_ref, wo_ref, zt_ref, lse_ref, own_in, other_in, low_ref,
    wq_ref, wk_ref, wv_ref, *rest, heads, span, rb, seq, last,
):
    if last:
        old_q, old_k, old_v, old_o = rest[:4]
        rest = rest[4:]
    own_ref, other_ref, dv_ref, gq_ref, gk_ref, gv_ref, go_ref, bias_ref, dk_sum, dv_sum, dqt_ref, dh_ref = rest
    length = q_ref.shape[0]
    lanes = heads * HD
    half = length // 2
    first = side[0] == 0
    dh_ref[:half, :] = jnp.where(first, own_in[...], other_in[...])
    dh_ref[half:, :] = jnp.where(first, other_in[...], own_in[...])
    dz = nt(dh_ref[...], wo_ref[...]).astype(BF16)
    dzt = dz.T
    q = q_ref[...] * score_scale
    qt = q.T
    kt = k_ref[...].T
    low_lane = lax.broadcasted_iota(jnp.int32, (1, 2 * HD), 1) < HD
    dk_sum[...] = jnp.zeros_like(dk_sum)
    dv_sum[...] = jnp.zeros_like(dv_sum)
    for p in range(length // span):
        for r in range(0, span, rb):
            bias_ref[:, r : r + rb] = span_bias(start[seq, p], size[seq, p], p * span, span, rb, r)
        before = p * span
        keys = before + span
        for r in range(0, span, rb):
            row0 = before + r
            dqs = []
            for lo in range(0, lanes, 2 * HD):
                hi = min(lo + 2 * HD, lanes)
                dks = []
                dvs = []
                for h in range(lo // HD, hi // HD):
                    qh = in_tile(qt[h * HD : (h + 1) * HD, row0 : row0 + rb], h, hi - lo)
                    dzh = in_tile(dzt[h * HD : (h + 1) * HD, row0 : row0 + rb], h, hi - lo)
                    lse = lse_ref[h : h + 1, row0 : row0 + rb]
                    scores = nn(k_ref[:keys, lo:hi], qh)
                    dprob = nn(v_ref[:keys, lo:hi], dzh)
                    prob = jnp.exp(scores[before:] + bias_ref[:, r : r + rb] - lse)
                    both = prob * dprob[before:]
                    delta = jnp.sum(both, axis=0, keepdims=True)
                    if p:
                        prob2 = jnp.exp(scores[:before] - lse)
                        both2 = prob2 * dprob[:before]
                        delta = delta + jnp.sum(both2, axis=0, keepdims=True)
                        prob_low = jnp.concatenate([prob2.astype(BF16), prob.astype(BF16)], 0)
                        ds = jnp.concatenate(
                            [(both2 - prob2 * delta).astype(BF16), (both - prob * delta).astype(BF16)], 0
                        )
                    else:
                        prob_low = prob.astype(BF16)
                        ds = (both - prob * delta).astype(BF16)
                    dqs.append((nn(kt[h * HD : (h + 1) * HD, :keys], ds) * score_scale).astype(BF16))
                    dks.append(nn(ds, q[row0 : row0 + rb, lo:hi]))
                    dvs.append(nn(prob_low, dz[row0 : row0 + rb, lo:hi]))
                if len(dks) == 2:
                    dk_sum[:keys, lo:hi] += jnp.where(low_lane, dks[0], dks[1])
                    dv_sum[:keys, lo:hi] += jnp.where(low_lane, dvs[0], dvs[1])
                else:
                    dk_sum[:keys, lo:hi] += dks[0]
                    dv_sum[:keys, lo:hi] += dvs[0]
            dqt_ref[:, row0 : row0 + rb] = jnp.concatenate(dqs, 0)
    dqt = dqt_ref[...]
    dk = dk_sum[...].astype(BF16)
    dv = dv_sum[...].astype(BF16)
    dv_ref[...] = dv
    dx = (nt(dqt.T, wq_ref[...]) + nt(dk, wk_ref[...]) + nt(dv, wv_ref[...])).astype(BF16)
    for part in range(2):
        store_half(side[0], part, slice(0, half), dx[part * half : (part + 1) * half], own_ref, other_ref)
    low = low_ref[...]
    gq = nn(dqt, low)
    gk = nn(dk.T, low)
    gv = nn(dv.T, low)
    go = nn(zt_ref[...], dh_ref[...])
    if last:
        gq_ref[...] = (gq + old_q[...]).T.astype(BF16)
        gk_ref[...] = (gk + old_k[...]).T.astype(BF16)
        gv_ref[...] = (gv + old_v[...]).T.astype(BF16)
        go_ref[...] = (go + old_o[...]).astype(BF16)
    else:
        gq_ref[...] = gq
        gk_ref[...] = gk
        gv_ref[...] = gv
        go_ref[...] = go


def attend_pull(side, start, size, q, k, v, wo, zt, lse, own, other, low, wq, wk, wv, old, heads, seq, last, rb=256):
    length, lanes = q.shape
    width = wo.shape[1]
    span = length // start.shape[1]
    rb = min(rb, span)
    ins = (q, k, v, wo, zt, lse, own, other, low, wq, wk, wv) + tuple(old)
    turned = (width, lanes) if last else (lanes, width)
    kind = BF16 if last else F32
    outs = (
        shaped(own.shape, BF16),
        shaped(own.shape, BF16),
        shaped((length, lanes), BF16),
        shaped(turned, kind),
        shaped(turned, kind),
        shaped(turned, kind),
        shaped((lanes, width), kind),
    )
    return pl.pallas_call(
        partial(attend_pull_body, heads=heads, span=span, rb=rb, seq=seq, last=last),
        out_shape=outs,
        grid_spec=pltpu.PrefetchScalarGridSpec(
            num_scalar_prefetch=3,
            grid=(1,),
            in_specs=[whole(i.shape) for i in ins],
            out_specs=tuple(whole(o.shape) for o in outs),
            scratch_shapes=[
                pltpu.VMEM((span, span), F32),
                pltpu.VMEM((length, lanes), F32),
                pltpu.VMEM((length, lanes), F32),
                pltpu.VMEM((lanes, length), BF16),
                pltpu.VMEM((length, width), BF16),
            ],
        ),
        compiler_params=params(),
        name="attend_pull",
    )(side, start, size, *ins)


def row_call(body, side, ins, outs, sums, seq, rows, name):
    half = next(array.shape[0] for array, kind in ins if kind == "half")
    steps = half // rows
    specs = []
    for array, kind in ins:
        if kind == "half":
            specs.append(pl.BlockSpec((rows, array.shape[1]), lambda i, s: (i, 0)))
        elif kind == "all":
            specs.append(
                pl.BlockSpec((rows, array.shape[1]), lambda i, s: ((2 * seq + s[0]) * steps + i, 0))
            )
        else:
            specs.append(whole(array.shape))
    out_specs = [pl.BlockSpec((rows, o.shape[1]), lambda i, s: (i, 0)) for o in outs]
    out_specs += [whole(o.shape) for o in sums]
    return pl.pallas_call(
        body,
        out_shape=tuple(outs) + tuple(sums),
        grid_spec=pltpu.PrefetchScalarGridSpec(
            num_scalar_prefetch=1, grid=(steps,), in_specs=specs, out_specs=tuple(out_specs)
        ),
        compiler_params=params(),
        name=name,
    )(side, *[array for array, _ in ins])


def norm_mid_body(side, part_ref, got_ref, x_ref, gain_ref, shift_ref, hidden_ref, low_ref):
    hidden = x_ref[...].astype(F32) + (part_ref[...].astype(F32) + got_ref[...].astype(F32))
    hidden_ref[...] = hidden
    normal, _ = normal_parts(hidden)
    low_ref[...] = (normal * gain_ref[...] + shift_ref[...]).astype(BF16)


def add_sums(sum_ref, values):
    @pl.when(pl.program_id(0) == 0)
    def _():
        sum_ref[...] = jnp.zeros_like(sum_ref)

    for row, value in enumerate(values):
        sum_ref[row : row + 1, :] += jnp.sum(value, axis=0, keepdims=True)


def norm_mid_pull_body(side, part_ref, got_ref, hidden_ref, cot_ref, gain_ref, dhidden_ref, low_ref, sum_ref):
    upstream = part_ref[...].astype(F32) + got_ref[...].astype(F32)
    normal, inverse = normal_parts(hidden_ref[...])
    cot = cot_ref[...].astype(F32)
    dhidden = cot + norm_pull(upstream, normal, inverse, gain_ref[...])
    dhidden_ref[...] = dhidden
    low_ref[...] = dhidden.astype(BF16)
    add_sums(sum_ref, (upstream * normal, upstream, cot))


def norm_first_pull_body(side, part_ref, got_ref, dhidden_ref, x_ref, gain_ref, out_ref, sum_ref):
    upstream = part_ref[...].astype(F32) + got_ref[...].astype(F32)
    normal, inverse = normal_parts(x_ref[...].astype(F32))
    out_ref[...] = dhidden_ref[...] + norm_pull(upstream, normal, inverse, gain_ref[...])
    add_sums(sum_ref, (upstream * normal, upstream))


def feed_body(side, x_ref, cot_ref, up_ref, bias_ref, down_ref, dx_ref, out_ref, active_ref, dpre_ref, sum_ref):
    pre = nn(x_ref[...], up_ref[...]) + bias_ref[...]
    root = 0.7978845608028654
    squared = pre * pre
    inner = jnp.tanh(root * pre * (1.0 + 0.044715 * squared))
    rise = 0.5 * (1.0 + inner)
    active = (pre * rise).astype(BF16)
    active_ref[...] = active
    slope = rise + 0.5 * pre * (1.0 - inner * inner) * (root * (1.0 + 3 * 0.044715 * squared))
    dpre = (nt(cot_ref[...], down_ref[...]) * slope).astype(BF16)
    dpre_ref[...] = dpre
    dx_ref[...] = nt(dpre, up_ref[...]).astype(BF16)
    out_ref[...] = nn(active, down_ref[...]).astype(BF16)
    add_sums(sum_ref, (dpre.astype(F32),))


def feed(side, x, cotangent, up, bias, down, seq, flip, rows=256):
    half, width = x.shape
    units = up.shape[1]
    steps = half // rows
    at = lambda i, s: (i, 0)
    if flip:
        cot_at = lambda i, s: ((2 * seq + 1 - s[0]) * steps + i, 0)
    else:
        cot_at = lambda i, s: ((2 * seq + s[0]) * steps + i, 0)
    return pl.pallas_call(
        feed_body,
        out_shape=(
            shaped((half, width), BF16),
            shaped((half, width), BF16),
            shaped((half, units), BF16),
            shaped((half, units), BF16),
            shaped((1, units), F32),
        ),
        grid_spec=pltpu.PrefetchScalarGridSpec(
            num_scalar_prefetch=1,
            grid=(steps,),
            in_specs=[
                pl.BlockSpec((rows, width), at),
                pl.BlockSpec((rows, width), cot_at),
                whole(up.shape),
                whole(bias.shape),
                whole(down.shape),
            ],
            out_specs=(
                pl.BlockSpec((rows, width), at),
                pl.BlockSpec((rows, width), at),
                pl.BlockSpec((rows, units), at),
                pl.BlockSpec((rows, units), at),
                whole((1, units)),
            ),
        ),
        compiler_params=params(),
        name="feed",
    )(side, x, cotangent, up, bias, down)


def outer_body(side, *refs, count):
    total = tn(refs[0][...], refs[count][...])
    for i in range(1, count):
        total = total + tn(refs[i][...], refs[count + i][...])
    refs[-1][...] = total.astype(BF16)


def outer_sum(side, lefts, rights, half, places=None):
    count = len(lefts)
    rows = lefts[0].shape[1]
    cols = rights[0].shape[1]
    specs = [whole(a.shape) for a in lefts]
    for i, array in enumerate(rights):
        if places is None:
            specs.append(whole(array.shape))
        else:
            seq, flip = places[i]
            if flip:
                specs.append(pl.BlockSpec((half, cols), lambda _, s, seq=seq: (2 * seq + 1 - s[0], 0)))
            else:
                specs.append(pl.BlockSpec((half, cols), lambda _, s, seq=seq: (2 * seq + s[0], 0)))
    return pl.pallas_call(
        partial(outer_body, count=count),
        out_shape=shaped((rows, cols), BF16),
        grid_spec=pltpu.PrefetchScalarGridSpec(
            num_scalar_prefetch=1, grid=(1,), in_specs=specs, out_specs=whole((rows, cols))
        ),
        compiler_params=params(),
        name="outer_sum",
    )(side, *lefts, *rights)


def xor_pairs(size, bit):
    return [(i, i ^ bit) for i in range(size)]


def xor_sum(value, axis):
    size = lax.axis_size(axis)
    bit = 1
    while bit < size:
        value = value + lax.ppermute(value, axis, xor_pairs(size, bit))
        bit *= 2
    return value


def on_device(
    inputs,
    first_values,
    piece_start,
    piece_length,
    cotangent,
    pre_attn_gain,
    pre_attn_bias,
    w_query,
    w_key,
    w_value,
    w_out,
    pre_mlp_gain,
    pre_mlp_bias,
    w_up,
    b_up,
    w_down,
    b_down,
):
    groups = lax.axis_size("tensor")
    member = lax.axis_index("tensor")
    local_heads = HEADS // groups
    columns = local_heads * HD
    is_fresh = member < VFRESH // local_heads
    core = member % 2
    tokens_dev, width = inputs.shape
    value_width = w_value.shape[1]
    seq_count = piece_start.shape[0]
    length = tokens_dev // seq_count
    half = length // 2
    side = core.astype(jnp.int32).reshape(1)
    fresh = is_fresh.astype(jnp.int32).reshape(1)
    seqs = range(seq_count)
    near = partial(lax.ppermute, axis_name="tensor", perm=xor_pairs(groups, 1))
    far = partial(lax.ppermute, axis_name="tensor", perm=xor_pairs(groups, 2))

    def row(vector):
        return vector.reshape(1, -1)

    def reduce_start(own, other):
        part = (own.astype(F32) + near(other).astype(F32)).astype(BF16)
        return part, far(part)

    def spread(own):
        got = near(own)
        return jnp.where(core == 0, own, got), jnp.where(core == 0, got, own)

    gain1, shift1, gain2, shift2 = map(row, (pre_attn_gain, pre_attn_bias, pre_mlp_gain, pre_mlp_bias))
    value_cols = lax.dynamic_slice_in_dim(
        w_value, jnp.minimum(member * columns, value_width - columns), columns, 1
    )
    first_cols = lax.dynamic_slice_in_dim(
        first_values, jnp.maximum(member * columns - value_width, 0), columns, 1
    )
    value_back = jnp.where(is_fresh, value_cols, jnp.zeros_like(value_cols))

    low, q, k, v, zt, lse, attn_part = [], [], [], [], [], [], []
    for s in seqs:
        a, b, c, d = project(
            fresh, inputs, gain1, shift1, w_query, w_key, value_cols, first_cols, s, length
        )
        low.append(a), q.append(b), k.append(c), v.append(d)
        z, l, own, other = attend(side, piece_start, piece_length, b, c, d, w_out, local_heads, s)
        zt.append(z), lse.append(l)
        attn_part.append(reduce_start(own, other))

    hidden, acts, dpres, mids, places, mlp_part, dmid_part, up_sums = [], [], [], [], [], [], [], []
    for s in seqs:
        part, got = attn_part[s]
        h, mid = row_call(
            norm_mid_body,
            side,
            [(part, "half"), (got, "half"), (inputs, "all"), (gain2, "vector"), (shift2, "vector")],
            [shaped((half, width), F32), shaped((half, width), BF16)],
            [],
            s,
            128,
            "norm_mid",
        )
        hidden.append(h)
        pieces = []
        for flip, piece in enumerate((mid, near(mid))):
            dx, out, act, dpre, sums = feed(
                side, piece, cotangent, w_up, row(b_up), w_down, s, flip
            )
            mids.append(piece), acts.append(act), dpres.append(dpre), places.append((s, flip))
            pieces.append((dx, out))
            up_sums.append(sums)
        dmid_part.append(reduce_start(pieces[0][0], pieces[1][0]))
        mlp_part.append((pieces[0][1], pieces[1][1]))

    grad_w_down = outer_sum(side, acts, [cotangent] * len(acts), half, places)
    grad_w_up = outer_sum(side, mids, dpres, half)
    grad_b_up = sum(up_sums)[0]

    dhidden, mid_sums, dlow, value_parts, in_part = [], [], [], [], []
    grads = ()
    for s in seqs:
        part, got = dmid_part[s]
        dh, dlo, sums = row_call(
            norm_mid_pull_body,
            side,
            [(part, "half"), (got, "half"), (hidden[s], "half"), (cotangent, "all"), (gain2, "vector")],
            [shaped((half, width), F32), shaped((half, width), BF16)],
            [shaped((3, width), F32)],
            s,
            128,
            "norm_mid_pull",
        )
        dhidden.append(dh), mid_sums.append(sums)
        own, other, dv, *grads = attend_pull(
            side, piece_start, piece_length, q[s], k[s], v[s], w_out, zt[s], lse[s], dlo, near(dlo), low[s],
            w_query, w_key, value_back, grads, local_heads, s, s == seq_count - 1,
        )
        value_parts.append(dv)
        in_part.append(reduce_start(own, other))

    outputs = []
    for s in seqs:
        part, got = reduce_start(*mlp_part[s])
        out = (hidden[s] + (part.astype(F32) + got.astype(F32)) + b_down).astype(BF16)
        outputs.extend(spread(out))
    outputs = jnp.concatenate(outputs, 0)

    grad_inputs, first_sums = [], []
    for s in seqs:
        part, got = in_part[s]
        g, sums = row_call(
            norm_first_pull_body,
            side,
            [(part, "half"), (got, "half"), (dhidden[s], "half"), (inputs, "all"), (gain1, "vector")],
            [shaped((half, width), F32)],
            [shaped((2, width), F32)],
            s,
            128,
            "norm_first_pull",
        )
        first_sums.append(sums)
        grad_inputs.extend(spread(g))
    grad_inputs = jnp.concatenate(grad_inputs, 0)

    fresh_members = VFRESH // local_heads
    firsts = []
    for s in seqs:
        got = lax.ppermute(
            value_parts[s], "tensor", [(i + fresh_members, i) for i in range(groups - fresh_members)]
        )
        mine = jnp.where(is_fresh, got, value_parts[s])
        got = near(mine)
        firsts.append(
            jnp.concatenate([jnp.where(core == 0, mine, got), jnp.where(core == 0, got, mine)], 1)
        )
    grad_first_values = jnp.concatenate(firsts, 0).astype(F32)

    grad_w_down, grad_w_up = lax.psum((grad_w_down, grad_w_up), "dp")
    grads, _ = lax.optimization_barrier((tuple(grads), grad_w_up[0, 0]))
    gq, gk, gv, go = lax.psum(grads, "dp")
    got = lax.ppermute(gv, "tensor", [(i, i + fresh_members) for i in range(groups - fresh_members)])
    mine = jnp.where(is_fresh, gv, got)
    got = near(mine)
    grad_w_value = jnp.concatenate(
        [jnp.where(core == 0, mine, got), jnp.where(core == 0, got, mine)], 1
    ).astype(F32)

    shared = jnp.concatenate([sum(first_sums), sum(mid_sums)], 0)
    shared = shared + near(shared)
    small = xor_sum(jnp.concatenate([shared, row(grad_b_up)], 0), "dp")

    return (
        outputs,
        grad_inputs,
        grad_first_values,
        small[0],
        small[1],
        gq.astype(F32),
        gk.astype(F32),
        grad_w_value,
        go.astype(F32),
        small[2],
        small[3],
        grad_w_up.astype(F32),
        small[5],
        grad_w_down.astype(F32),
        small[4],
    )


def solution(mesh):
    return jax.shard_map(
        on_device,
        mesh=mesh,
        in_specs=(
            P("dp", None),
            P("dp", None),
            P("dp", None),
            P("dp", None),
            P("dp", None),
            P(),
            P(),
            P(None, "tensor"),
            P(None, "tensor"),
            P(),
            P("tensor", None),
            P(),
            P(),
            P(None, "tensor"),
            P("tensor"),
            P("tensor", None),
            P(),
        ),
        out_specs=(
            P("dp", None),
            P("dp", None),
            P("dp", None),
            P(),
            P(),
            P(None, "tensor"),
            P(None, "tensor"),
            P(),
            P("tensor", None),
            P(),
            P(),
            P(None, "tensor"),
            P("tensor"),
            P("tensor", None),
            P(),
        ),
        check_vma=False,
    )
```

time: 809 us -> 436 us (0.54)
  waiting for transfers between devices: 460 us -> 201 us
  matrix products: 134 us -> 0 us
  Pallas kernels: 0 us -> 134 us
  local copies, waits for them, and re-layouts: 68.7 us -> 20.6 us
  other arithmetic: 76.1 us -> 28.4 us
  blocking collectives: 38.2 us -> 0 us
  starting transfers between devices: 1.2 us -> 29.6 us
    psum x4 -> x1, waiting for transfers between devices: 460 us -> 69 us  [on_device(): gq, gk, gv, go = lax.psum(grads, 'dp')]
    pallas_call x0 -> x18, Pallas kernels: none -> 134 us  [the longest x2 37.4 us: attend_pull(): pl.pallas_call(partial(attend_pull_body, heads=heads, span=span, rb=rb, s...]
    dot_general x46 -> x0, matrix products: 134 us -> none  [the longest x6 23.2 us: transposed_times(): lax.dot_general(left, right, (((0,), (0,)), ((), ())), preferred_element_...]
    ppermute x0 -> x34, waiting for transfers between devices: none -> 132 us  [the longest x8 117 us: reduce_start(): return (part, far(part))]
    psum x1 -> x0, blocking collectives: 38.2 us -> none  [on_device(): lax.psum((grad_attn_gain, grad_attn_bias, grad_w_query, grad_w_key, grad_...]
    reduce_sum x12 -> x0, other arithmetic: 36.6 us -> none  [the longest x2 12.8 us: norm_backward(): jnp.sum(upstream * normal_part, axis=0)]
    ppermute x0 -> x34, starting transfers between devices: none -> 29.5 us  [the longest x8 11.3 us: reduce_start(): return (part, far(part))]
    dynamic_slice x29 -> x1, local copies, waits for them, and re-layouts: 15.3 us -> 1.4 us  [on_device(): lax.dynamic_slice_in_dim(first_values, jnp.maximum(member * columns - val...]
  transfers between devices with their start and end apart: 6 -> 35, of which waited for: 4 -> 14; matrix products, arithmetic and copies ran while one was open for 8% -> 7% of each run, Pallas kernels for 0% -> 28%
where the time goes in v1:
time: 436 us; the launch traced here: 428 us
  waiting for transfers between devices  201 us (46%)
  Pallas kernels  134 us (31%)
  starting transfers between devices  29.6 us (7%)
  other arithmetic  28.4 us (7%)
  local copies, waits for them, and re-layouts  20.6 us (5%)
  between operations  14.8 us (3%)
    ppermute x8, waiting for transfers between devices, reduce_start(): return (part, far(part))  117 us
    psum x1, waiting for transfers between devices, on_device(): gq, gk, gv, go = lax.psum(grads, 'dp')  69 us
    pallas_call x2, Pallas kernels, attend_pull(): pl.pallas_call(partial(attend_pull_body, heads=heads, span=span, rb=rb, s...  37.4 us
    pallas_call x6, Pallas kernels, row_call(): pl.pallas_call(body, out_shape=tuple(outs) + tuple(sums), grid_spec=pltpu...  28.2 us
    pallas_call x4, Pallas kernels, feed(): pl.pallas_call(feed_body, out_shape=(shaped((half, width), BF16), shaped(...  24.9 us
    pallas_call x2, Pallas kernels, attend(): pl.pallas_call(partial(attend_body, heads=heads, span=span, rb=rb, seq=se...  17.9 us
    unnamed x96, local copies, waits for them, and re-layouts  14.2 us
    pallas_call x2, Pallas kernels, outer_sum(): pl.pallas_call(partial(outer_body, count=count), out_shape=shaped((rows,...  12.9 us
  transfers between devices with their start and end apart: 35, of which 14 were waited for; matrix products, arithmetic and copies ran while one was open for 7% of the time, Pallas kernels for 28%

profile of v1, /device:TPU:0, one launch (start us, length us, event | category | flops | bytes accessed | tf_op | source)
XLA Modules:
  0.0 428.0 jit_solution(16299287345366237951)
XLA Ops:
  7.3 2.0 copy.32.wq_ref
  9.3 1.9 copy.33.wk_ref
  11.2 1.3 reshape.60.gain_ref
  12.5 1.3 reshape.61.shift_ref
  13.7 1.1 broadcast_select_fusion.17
  14.9 1.4 constant_dynamic-slice_fusion.first_ref
  16.3 6.4 %project.2 = (bf16[1024,768]{1,0:T(8,128)(2,1)}, bf16[1024,192]{1,0:T(8,128)(2,1)}, bf16[1024,192]{1,0:T(8,128)(2,1)}, bf16[1024,192]{1,0:T(8,128)(2,1)}) custom-call(s32[1]{0:T(128)} %bitcast.1.fresh, bf16[2048,768]{1,0:T(8,128)(2,1)} %x_ref.11, f32[1,768]{1,0:T(1,128)} %reshape.60.gain_ref, f32[1,768]{1,0:T(1,128)} %reshape.61.shift_ref, ...), custom_call_target="tpu_custom_call" | custom-call | tf_op jit(solution)/shard_map/project/pallas_call | solution.py:83
  22.7 8.8 %attend.2 = (bf16[192,1024]{1,0:T(8,128)(2,1)}, f32[3,1024]{1,0:T(4,128)}, bf16[512,768]{1,0:T(8,128)(2,1)}, bf16[512,768]{1,0:T(8,128)(2,1)}) custom-call(s32[1]{0:T(128)} %bitcast.side, s32[2,2]{1,0:T(2,128)} %start.7, s32[2,2]{1,0:T(2,128)} %size.7, bf16[1024,192]{1,0:T(8,128)(2,1)} %get-tuple-element.83.q_ref, ...), custom_call_target="tpu_custom_call" | custom-call | tf_op jit(solution)/shard_map/attend/pallas_call | solution.py:177
  31.9 6.4 %project.3 = (bf16[1024,768]{1,0:T(8,128)(2,1)}, bf16[1024,192]{1,0:T(8,128)(2,1)}, bf16[1024,192]{1,0:T(8,128)(2,1)}, bf16[1024,192]{1,0:T(8,128)(2,1)}) custom-call(s32[1]{0:T(128)} %bitcast.1.fresh, bf16[2048,768]{1,0:T(8,128)(2,1)} %x_ref.11, f32[1,768]{1,0:T(1,128)} %reshape.60.gain_ref, f32[1,768]{1,0:T(1,128)} %reshape.61.shift_ref, ...), custom_call_target="tpu_custom_call" | custom-call | tf_op jit(solution)/shard_map/project/pallas_call | solution.py:83
  38.3 9.1 %attend.3 = (bf16[192,1024]{1,0:T(8,128)(2,1)}, f32[3,1024]{1,0:T(4,128)}, bf16[512,768]{1,0:T(8,128)(2,1)}, bf16[512,768]{1,0:T(8,128)(2,1)}) custom-call(s32[1]{0:T(128)} %bitcast.side, s32[2,2]{1,0:T(2,128)} %start.7, s32[2,2]{1,0:T(2,128)} %size.7, bf16[1024,192]{1,0:T(8,128)(2,1)} %get-tuple-element.92.q_ref, ...), custom_call_target="tpu_custom_call" | custom-call | tf_op jit(solution)/shard_map/attend/pallas_call | solution.py:177
  47.7 1.5 collective-permute-start.1
  50.1 1.1 collective-permute-start.7
  52.4 15.8 %collective-permute-done.1.got_ref = bf16[512,768]{1,0:T(8,128)(2,1)S(1)} collective-permute-done((bf16[512,768]{1,0:T(8,128)(2,1)S(1)}, bf16[512,768]{1,0:T(8,128)(2,1)S(1)}, u32[]{:S(2)}, u32[]{:S(2)}) %collective-permute-start.1) | collective-permute-done | bytes 786464 | tf_op jit(solution)/shard_map/ppermute | solution.py:530
  69.0 4.1 norm_mid.2
  73.2 11.3 %collective-permute-done.7.got_ref = bf16[512,768]{1,0:T(8,128)(2,1)S(1)} collective-permute-done((bf16[512,768]{1,0:T(8,128)(2,1)S(1)}, bf16[512,768]{1,0:T(8,128)(2,1)S(1)}, u32[]{:S(2)}, u32[]{:S(2)}) %collective-permute-start.7) | collective-permute-done | bytes 786464 | tf_op jit(solution)/shard_map/ppermute | solution.py:530
  85.4 4.1 norm_mid.3
  91.0 6.2 %feed.5 = (bf16[512,768]{1,0:T(8,128)(2,1)}, bf16[512,768]{1,0:T(8,128)(2,1)}, bf16[512,768]{1,0:T(8,128)(2,1)}, bf16[512,768]{1,0:T(8,128)(2,1)}, f32[1,768]{1,0:T(1,128)}) custom-call(s32[1]{0:T(128)} %bitcast.side, bf16[512,768]{1,0:T(8,128)(2,1)} %copy-done.8, bf16[2048,768]{1,0:T(8,128)(2,1)} %refs_7_.1, bf16[768,768]{1,0:T(8,128)(2,1)} %up_ref.7, ...), custom_call_target="tpu_custom_call" | custom-call | tf_op jit(solution)/shard_map/feed/pallas_call | solution.py:412
  98.7 6.2 %feed.7 = (bf16[512,768]{1,0:T(8,128)(2,1)}, bf16[512,768]{1,0:T(8,128)(2,1)}, bf16[512,768]{1,0:T(8,128)(2,1)}, bf16[512,768]{1,0:T(8,128)(2,1)}, f32[1,768]{1,0:T(1,128)}) custom-call(s32[1]{0:T(128)} %bitcast.side, bf16[512,768]{1,0:T(8,128)(2,1)} %copy-done.9, bf16[2048,768]{1,0:T(8,128)(2,1)} %refs_7_.1, bf16[768,768]{1,0:T(8,128)(2,1)} %up_ref.7, ...), custom_call_target="tpu_custom_call" | custom-call | tf_op jit(solution)/shard_map/feed/pallas_call | solution.py:412
  105.4 6.2 %feed.6 = (bf16[512,768]{1,0:T(8,128)(2,1)}, bf16[512,768]{1,0:T(8,128)(2,1)}, bf16[512,768]{1,0:T(8,128)(2,1)}, bf16[512,768]{1,0:T(8,128)(2,1)}, f32[1,768]{1,0:T(1,128)}) custom-call(s32[1]{0:T(128)} %bitcast.side, bf16[512,768]{1,0:T(8,128)(2,1)} %get-tuple-element.98.x_ref.refs_2_, bf16[2048,768]{1,0:T(8,128)(2,1)} %refs_7_.1, bf16[768,768]{1,0:T(8,128)(2,1)} %up_ref.7, ...), custom_call_target="tpu_custom_call" | custom-call | tf_op jit(solution)/shard_map/feed/pallas_call | solution.py:412
  111.6 6.3 %feed.4 = (bf16[512,768]{1,0:T(8,128)(2,1)}, bf16[512,768]{1,0:T(8,128)(2,1)}, bf16[512,768]{1,0:T(8,128)(2,1)}, bf16[512,768]{1,0:T(8,128)(2,1)}, f32[1,768]{1,0:T(1,128)}) custom-call(s32[1]{0:T(128)} %bitcast.side, bf16[512,768]{1,0:T(8,128)(2,1)} %get-tuple-element.89.x_ref.refs_0_, bf16[2048,768]{1,0:T(8,128)(2,1)} %refs_7_.1, bf16[768,768]{1,0:T(8,128)(2,1)} %up_ref.7, ...), custom_call_target="tpu_custom_call" | custom-call | tf_op jit(solution)/shard_map/feed/pallas_call | solution.py:412
  118.1 1.4 add_convert_fusion.3.part_ref
  119.5 1.0 collective-permute-start.13
  120.7 1.2 collective-permute-start.19
  123.3 1.2 collective-permute-start.4
  124.4 15.5 %collective-permute-done.13.got_ref = bf16[512,768]{1,0:T(8,128)(2,1)S(1)} collective-permute-done((bf16[512,768]{1,0:T(8,128)(2,1)S(1)}, bf16[512,768]{1,0:T(8,128)(2,1)S(1)}, u32[]{:S(2)}, u32[]{:S(2)}) %collective-permute-start.13) | collective-permute-done | bytes 786464 | tf_op jit(solution)/shard_map/ppermute | solution.py:530
  140.9 5.0 %norm_mid_pull.2 = (f32[512,768]{1,0:T(8,128)}, bf16[512,768]{1,0:T(8,128)(2,1)}, f32[3,768]{1,0:T(4,128)}) custom-call(s32[1]{0:T(128)} %bitcast.side, bf16[512,768]{1,0:T(8,128)(2,1)} %copy-done.7, bf16[512,768]{1,0:T(8,128)(2,1)} %copy-done.19, f32[512,768]{1,0:T(8,128)} %get-tuple-element.88.hidden_ref, bf16[2048,768]{1,0:T(8,128)(2,1)} %refs_7_.1, ...), custom_call_target="tpu_custom_call" | custom-call | tf_op jit(solution)/shard_map/norm_mid_pull/pallas_call | solution.py:343
  146.0 10.8 %collective-permute-done.19.got_ref = bf16[512,768]{1,0:T(8,128)(2,1)S(1)} collective-permute-done((bf16[512,768]{1,0:T(8,128)(2,1)S(1)}, bf16[512,768]{1,0:T(8,128)(2,1)S(1)}, u32[]{:S(2)}, u32[]{:S(2)}) %collective-permute-start.19) | collective-permute-done | bytes 786464 | tf_op jit(solution)/shard_map/ppermute | solution.py:530
  157.7 5.5 %norm_mid_pull.3 = (f32[512,768]{1,0:T(8,128)}, bf16[512,768]{1,0:T(8,128)(2,1)}, f32[3,768]{1,0:T(4,128)}) custom-call(s32[1]{0:T(128)} %bitcast.side, bf16[512,768]{1,0:T(8,128)(2,1)} %copy-done.4, bf16[512,768]{1,0:T(8,128)(2,1)} %copy-done.16, f32[512,768]{1,0:T(8,128)} %get-tuple-element.97.hidden_ref, bf16[2048,768]{1,0:T(8,128)(2,1)} %refs_7_.1, ...), custom_call_target="tpu_custom_call" | custom-call | tf_op jit(solution)/shard_map/norm_mid_pull/pallas_call | solution.py:343
  163.3 10.5 %collective-permute-done.10 = bf16[512,768]{1,0:T(8,128)(2,1)} collective-permute-done((bf16[512,768]{1,0:T(8,128)(2,1)S(1)}, bf16[512,768]{1,0:T(8,128)(2,1)}, u32[]{:S(2)}, u32[]{:S(2)}) %collective-permute-start.10) | collective-permute-done | bytes 786464 | tf_op jit(solution)/shard_map/ppermute | solution.py:530
  173.8 16.2 %collective-permute-done.4 = bf16[512,768]{1,0:T(8,128)(2,1)} collective-permute-done((bf16[512,768]{1,0:T(8,128)(2,1)S(1)}, bf16[512,768]{1,0:T(8,128)(2,1)}, u32[]{:S(2)}, u32[]{:S(2)}) %collective-permute-start.4) | collective-permute-done | bytes 786464 | tf_op jit(solution)/shard_map/ppermute | solution.py:530
  190.0 1.9 add_convert_fusion.7
  192.1 18.3 %attend_pull.2 = (bf16[512,768]{1,0:T(8,128)(2,1)}, bf16[512,768]{1,0:T(8,128)(2,1)}, bf16[1024,192]{1,0:T(8,128)(2,1)}, f32[192,768]{1,0:T(8,128)}, f32[192,768...) custom-call(s32[1]{0:T(128)} %bitcast.side, s32[2,2]{1,0:T(2,128)} %start.7, s32[2,2]{1,0:T(2,128)} %size.7, ...), custom_call_target="tpu_custom_call" | custom-call | tf_op jit(solution)/shard_map/attend_pull/pallas_call | solution.py:307
  210.8 6.5 %outer_sum.3 = bf16[768,768]{1,0:T(8,128)(2,1)} custom-call(s32[1]{0:T(128)} %bitcast.side, bf16[512,768]{1,0:T(8,128)(2,1)} %get-tuple-element.147.refs_0_, bf16[512,768]{1,0:T(8,128)(2,1)} %get-tuple-element.148.refs_1_, bf16[512,768]{1,0:T(8,128)(2,1)} %get-tuple-element.149.refs_2_, bf16[512,768]{1,0:T(8,128)(2,1)} %get-tuple-element.150.refs_3_, ...), custom_call_target="tpu_custom_call" | custom-call | tf_op jit(solution)/shard_map/outer_sum/pallas_call | solution.py:465
  217.3 6.5 %outer_sum.2 = bf16[768,768]{1,0:T(8,128)(2,1)} custom-call(s32[1]{0:T(128)} %bitcast.side, bf16[512,768]{1,0:T(8,128)(2,1)} %get-tuple-element.89.x_ref.refs_0_, bf16[512,768]{1,0:T(8,128)(2,1)} %copy-done.8, bf16[512,768]{1,0:T(8,128)(2,1)} %get-tuple-element.98.x_ref.refs_2_, bf16[512,768]{1,0:T(8,128)(2,1)} %copy-done.9, ...), custom_call_target="tpu_custom_call" | custom-call | tf_op jit(solution)/shard_map/outer_sum/pallas_call | solution.py:465
  224.7 19.1 %attend_pull.3 = (bf16[512,768]{1,0:T(8,128)(2,1)}, bf16[512,768]{1,0:T(8,128)(2,1)}, bf16[1024,192]{1,0:T(8,128)(2,1)}, bf16[768,192]{1,0:T(8,128)(2,1)}, bf16[...) custom-call(s32[1]{0:T(128)} %bitcast.side, s32[2,2]{1,0:T(2,128)} %start.7, s32[2,2]{1,0:T(2,128)} %size.7, ...), custom_call_target="tpu_custom_call" | custom-call | tf_op jit(solution)/shard_map/attend_pull/pallas_call | solution.py:307
  244.4 1.3 collective-permute-start.24
  245.8 1.4 collective-permute-start.26
  247.2 1.2 broadcast_select_fusion.7
  248.5 1.4 add_convert_fusion.2.part_ref
  249.9 4.3 %collective-permute-start.16 = (bf16[512,768]{1,0:T(8,128)(2,1)S(1)}, bf16[512,768]{1,0:T(8,128)(2,1)S(1)}, u32[]{:S(2)}, u32[]{:S(2)}) collective-permute-start(bf16[512,768]{1,0:T(8,128)(2,1)S(1)} %add_convert_fusion.2.part_ref), channel_id=1, source_target_pairs={{0,2},{1,3},{2,0},{3,1},{4,6},{5,7},{6,4},{7,5},{8,10},{9,11},{10,... | collective-permute-start | bytes 2359304 | tf_op jit(solution)/shard_map/ppermute | solution.py:530
  254.5 1.5 broadcast_select_fusion.5
  256.1 1.8 pad_maximum_fusion.1
  257.9 3.5 collective-permute-done.24
  261.4 1.1 broadcast_select_fusion.9
  262.6 26.8 %collective-permute-done.16.got_ref = bf16[512,768]{1,0:T(8,128)(2,1)S(1)} collective-permute-done((bf16[512,768]{1,0:T(8,128)(2,1)S(1)}, bf16[512,768]{1,0:T(8,128)(2,1)S(1)}, u32[]{:S(2)}, u32[]{:S(2)}) %collective-permute-start.16) | collective-permute-done | bytes 786464 | tf_op jit(solution)/shard_map/ppermute | solution.py:530
  290.3 4.7 %norm_first_pull.2 = (f32[512,768]{1,0:T(8,128)}, f32[2,768]{1,0:T(2,128)}) custom-call(s32[1]{0:T(128)} %bitcast.side, bf16[512,768]{1,0:T(8,128)(2,1)} %copy-done.5, bf16[512,768]{1,0:T(8,128)(2,1)} %copy-done.17, f32[512,768]{1,0:T(8,128)} %get-tuple-element.109.dhidden_ref, bf16[2048,768]{1,0:T(8,128)(2,1)} %x_ref.11, f32[1,768]{1,0:T(1,128)} %reshape.60.gain_ref), custom_call_target="tpu_custom_call" | custom-call | tf_op jit(solution)/shard_map/norm_first_pull/pallas_call | solution.py:343
  295.0 10.3 %collective-permute-done.22.got_ref = bf16[512,768]{1,0:T(8,128)(2,1)S(1)} collective-permute-done((bf16[512,768]{1,0:T(8,128)(2,1)S(1)}, bf16[512,768]{1,0:T(8,128)(2,1)S(1)}, u32[]{:S(2)}, u32[]{:S(2)}) %collective-permute-start.22) | collective-permute-done | bytes 786464 | tf_op jit(solution)/shard_map/ppermute | solution.py:530
  306.2 4.8 %norm_first_pull.3 = (f32[512,768]{1,0:T(8,128)}, f32[2,768]{1,0:T(2,128)}) custom-call(s32[1]{0:T(128)} %bitcast.side, bf16[512,768]{1,0:T(8,128)(2,1)} %copy-done.6, bf16[512,768]{1,0:T(8,128)(2,1)} %copy-done.18, f32[512,768]{1,0:T(8,128)} %get-tuple-element.123.dhidden_ref, bf16[2048,768]{1,0:T(8,128)(2,1)} %x_ref.11, f32[1,768]{1,0:T(1,128)} %reshape.60.gain_ref), custom_call_target="tpu_custom_call" | custom-call | tf_op jit(solution)/shard_map/norm_first_pull/pallas_call | solution.py:343
  312.3 1.1 broadcast_select_fusion.8
  314.1 2.6 collective-permute-start.29
  316.7 1.7 collective-permute-done.29
  318.5 2.1 collective-permute-start.30
  320.7 1.8 collective-permute-done.30
  322.5 2.9 collective-permute-start.31
  325.5 2.2 maximum_convert_fusion
  328.5 69.0 %all-reduce.3.cloned.1.call-done = (bf16[768,192]{1,0:T(8,128)(2,1)}, bf16[768,192]{1,0:T(8,128)(2,1)}, bf16[768,192]{1,0:T(8,128)(2,1)}, bf16[192,768]{1,0:T(8,...) async-done(((bf16[768,192]{1,0:T(8,128)(2,1)}, bf16[768,192]{1,0:T(8,128)(2,1)}, bf16[768,192]{1,0:T(8,128)(2,1)}, bf16[192,768]{1,0:T(8,128)(2,1)}, ...) | async-done | bytes 3538960 | tf_op jit(solution)/shard_map/psum | solution.py:645
  397.5 3.5 collective-permute-start.32
  401.1 2.1 broadcast_select_fusion.1
  403.2 6.4 %collective-permute-done.32 = bf16[768,192]{1,0:T(8,128)(2,1)S(1)} collective-permute-done((bf16[768,192]{1,0:T(8,128)(2,1)}, bf16[768,192]{1,0:T(8,128)(2,1)S(1)}, u32[]{:S(2)}, u32[]{:S(2)}) %collective-permute-start.32) | collective-permute-done | bytes 294944 | tf_op jit(solution)/shard_map/ppermute | solution.py:646
  409.7 2.9 pad_maximum_fusion
  412.6 1.6 convert_element_type.147
  414.3 1.6 convert_element_type.148
  418.7 1.1 broadcast_select_fusion.15
  419.7 1.2 maximum_convert_fusion.1
  (164 shorter events, 22.2 us)
Async XLA Ops:
  7.2 7.7 %copy-start = (bf16[2048,384]{1,0:T(8,128)(2,1)S(1)}, bf16[2048,384]{1,0:T(8,128)(2,1)}, u32[]{:S(2)}) copy-start(bf16[2048,384]{1,0:T(8,128)(2,1)} %param.18) | copy-start | bytes 4718596
  7.2 6.5 %copy-start.33 = (bf16[768,384]{1,0:T(8,128)(2,1)S(1)}, bf16[768,384]{1,0:T(8,128)(2,1)}, u32[]{:S(2)}) copy-start(bf16[768,384]{1,0:T(8,128)(2,1)} %param.26) | copy-start | bytes 1769476
  7.2 390.3 %all-reduce.3.cloned.1.call-start = ((), (), s32[]{:S(2)}) async-start(), calls=%async_computation | async-start | bytes 7667712 | tf_op jit(solution)/shard_map/psum | solution.py:645
  31.4 16.0 %collective-permute-start = (bf16[512,768]{1,0:T(8,128)(2,1)}, bf16[512,768]{1,0:T(8,128)(2,1)S(1)}, u32[]{:S(2)}, u32[]{:S(2)}) collective-permute-start(bf16[512,768]{1,0:T(8,128)(2,1)} %get-tuple-element.87), channel_id=1, source_target_pairs={{0,1},{1,0},{2,3},{3,2},{4,5},{5,4},{6,7},{7,6},{8,9},{9,8},{10,11... | collective-permute-start | bytes 2359304 | tf_op jit(solution)/shard_map/ppermute | solution.py:529
  38.3 9.1 %copy-start.25 = (bf16[512,768]{1,0:T(8,128)(2,1)S(1)}, bf16[512,768]{1,0:T(8,128)(2,1)}, u32[]{:S(2)}) copy-start(bf16[512,768]{1,0:T(8,128)(2,1)} %get-tuple-element.86) | copy-start | bytes 2359300
  47.4 2.5 collective-permute-start.6
  47.6 20.5 %copy-start.11 = (bf16[512,768]{1,0:T(8,128)(2,1)}, bf16[512,768]{1,0:T(8,128)(2,1)S(1)}, u32[]{:S(2)}) copy-start(bf16[512,768]{1,0:T(8,128)(2,1)S(1)} %add_convert_fusion.9.part_ref) | copy-start | bytes 2359300
  47.6 3.6 copy-start.38
  47.7 4.1 copy-start.39
  47.7 20.5 %collective-permute-start.1 = (bf16[512,768]{1,0:T(8,128)(2,1)S(1)}, bf16[512,768]{1,0:T(8,128)(2,1)S(1)}, u32[]{:S(2)}, u32[]{:S(2)}) collective-permute-start(bf16[512,768]{1,0:T(8,128)(2,1)S(1)} %add_convert_fusion.9.part_ref), channel_id=1, source_target_pairs={{0,2},{1,3},{2,0},{3,1},{4,6},{5,7},{6,4},{7,5},{8,10},{9,11},{10,... | collective-permute-start | bytes 2359304 | tf_op jit(solution)/shard_map/ppermute | solution.py:530
  50.1 23.0 %copy-start.10 = (bf16[512,768]{1,0:T(8,128)(2,1)}, bf16[512,768]{1,0:T(8,128)(2,1)S(1)}, u32[]{:S(2)}) copy-start(bf16[512,768]{1,0:T(8,128)(2,1)S(1)} %add_convert_fusion.6.part_ref) | copy-start | bytes 2359300
  50.1 34.4 %collective-permute-start.7 = (bf16[512,768]{1,0:T(8,128)(2,1)S(1)}, bf16[512,768]{1,0:T(8,128)(2,1)S(1)}, u32[]{:S(2)}, u32[]{:S(2)}) collective-permute-start(bf16[512,768]{1,0:T(8,128)(2,1)S(1)} %add_convert_fusion.6.part_ref), channel_id=1, source_target_pairs={{0,2},{1,3},{2,0},{3,1},{4,6},{5,7},{6,4},{7,5},{8,10},{9,11},{10,... | collective-permute-start | bytes 2359304 | tf_op jit(solution)/shard_map/ppermute | solution.py:530
  73.1 16.4 %copy-start.40 = (f32[768]{0:T(1024)S(1)}, f32[768]{0:T(1024)}, u32[]{:S(2)}) copy-start(f32[768]{0:T(1024)} %param.31) | copy-start | bytes 9220
  73.1 17.0 %collective-permute-start.2 = (bf16[512,768]{1,0:T(8,128)(2,1)}, bf16[512,768]{1,0:T(8,128)(2,1)S(1)}, u32[]{:S(2)}, u32[]{:S(2)}) collective-permute-start(bf16[512,768]{1,0:T(8,128)(2,1)} %get-tuple-element.89.x_ref.refs_0_), channel_id=1, source_target_pairs={{0,1},{1,0},{2,3},{3,2},{4,5},{5,4},{6,7},{7,6},{8,9},{9,8},{10,11... | collective-permute-start | bytes 2359304 | tf_op jit(solution)/shard_map/ppermute | solution.py:570
  89.5 8.3 %collective-permute-start.8 = (bf16[512,768]{1,0:T(8,128)(2,1)}, bf16[512,768]{1,0:T(8,128)(2,1)S(1)}, u32[]{:S(2)}, u32[]{:S(2)}) collective-permute-start(bf16[512,768]{1,0:T(8,128)(2,1)} %get-tuple-element.98.x_ref.refs_2_), channel_id=1, source_target_pairs={{0,1},{1,0},{2,3},{3,2},{4,5},{5,4},{6,7},{7,6},{8,9},{9,8},{10,11... | collective-permute-start | bytes 2359304 | tf_op jit(solution)/shard_map/ppermute | solution.py:570
  97.2 20.8 %collective-permute-start.12 = (bf16[512,768]{1,0:T(8,128)(2,1)}, bf16[512,768]{1,0:T(8,128)(2,1)S(1)}, u32[]{:S(2)}, u32[]{:S(2)}) collective-permute-start(bf16[512,768]{1,0:T(8,128)(2,1)} %get-tuple-element.104), channel_id=1, source_target_pairs={{0,1},{1,0},{2,3},{3,2},{4,5},{5,4},{6,7},{7,6},{8,9},{9,8},{10,11... | collective-permute-start | bytes 2359304 | tf_op jit(solution)/shard_map/ppermute | solution.py:529
  104.9 15.6 %collective-permute-start.18 = (bf16[512,768]{1,0:T(8,128)(2,1)}, bf16[512,768]{1,0:T(8,128)(2,1)S(1)}, u32[]{:S(2)}, u32[]{:S(2)}) collective-permute-start(bf16[512,768]{1,0:T(8,128)(2,1)} %get-tuple-element.114), channel_id=1, source_target_pairs={{0,1},{1,0},{2,3},{3,2},{4,5},{5,4},{6,7},{7,6},{8,9},{9,8},{10,11... | collective-permute-start | bytes 2359304 | tf_op jit(solution)/shard_map/ppermute | solution.py:529
  104.9 17.0 %collective-permute-start.9 = (bf16[512,768]{1,0:T(8,128)(2,1)}, bf16[512,768]{1,0:T(8,128)(2,1)S(1)}, u32[]{:S(2)}, u32[]{:S(2)}) collective-permute-start(bf16[512,768]{1,0:T(8,128)(2,1)} %get-tuple-element.100), channel_id=1, source_target_pairs={{0,1},{1,0},{2,3},{3,2},{4,5},{5,4},{6,7},{7,6},{8,9},{9,8},{10,11... | collective-permute-start | bytes 2359304 | tf_op jit(solution)/shard_map/ppermute | solution.py:529
  111.6 6.3 %copy-start.45 = (bf16[512,768]{1,0:T(8,128)(2,1)S(1)}, bf16[512,768]{1,0:T(8,128)(2,1)}, u32[]{:S(2)}) copy-start(bf16[512,768]{1,0:T(8,128)(2,1)} %get-tuple-element.91) | copy-start | bytes 2359300
  117.9 2.6 copy-start.24
  117.9 5.1 %collective-permute-start.3 = (bf16[512,768]{1,0:T(8,128)(2,1)S(1)}, bf16[512,768]{1,0:T(8,128)(2,1)S(1)}, u32[]{:S(2)}, u32[]{:S(2)}) collective-permute-start(bf16[512,768]{1,0:T(8,128)(2,1)S(1)} %copy-done.45), channel_id=1, source_target_pairs={{0,1},{1,0},{2,3},{3,2},{4,5},{5,4},{6,7},{7,6},{8,9},{9,8},{10,11... | collective-permute-start | bytes 2359304 | tf_op jit(solution)/shard_map/ppermute | solution.py:529
  119.5 2.6 copy-start.7
  119.5 20.5 %collective-permute-start.13 = (bf16[512,768]{1,0:T(8,128)(2,1)S(1)}, bf16[512,768]{1,0:T(8,128)(2,1)S(1)}, u32[]{:S(2)}, u32[]{:S(2)}) collective-permute-start(bf16[512,768]{1,0:T(8,128)(2,1)S(1)} %add_convert_fusion.3.part_ref), channel_id=1, source_target_pairs={{0,2},{1,3},{2,0},{3,1},{4,6},{5,7},{6,4},{7,5},{8,10},{9,11},{10,... | collective-permute-start | bytes 2359304 | tf_op jit(solution)/shard_map/ppermute | solution.py:530
  120.7 2.6 copy-start.4
  120.7 36.1 %collective-permute-start.19 = (bf16[512,768]{1,0:T(8,128)(2,1)S(1)}, bf16[512,768]{1,0:T(8,128)(2,1)S(1)}, u32[]{:S(2)}, u32[]{:S(2)}) collective-permute-start(bf16[512,768]{1,0:T(8,128)(2,1)S(1)} %add_convert_fusion.1.part_ref), channel_id=1, source_target_pairs={{0,2},{1,3},{2,0},{3,1},{4,6},{5,7},{6,4},{7,5},{8,10},{9,11},{10,... | collective-permute-start | bytes 2359304 | tf_op jit(solution)/shard_map/ppermute | solution.py:530
  122.1 51.7 %collective-permute-start.10 = (bf16[512,768]{1,0:T(8,128)(2,1)S(1)}, bf16[512,768]{1,0:T(8,128)(2,1)}, u32[]{:S(2)}, u32[]{:S(2)}) collective-permute-start(bf16[512,768]{1,0:T(8,128)(2,1)S(1)} %add_convert_fusion.5), channel_id=1, source_target_pairs={{0,2},{1,3},{2,0},{3,1},{4,6},{5,7},{6,4},{7,5},{8,10},{9,11},{10,... | collective-permute-start | bytes 2359304 | tf_op jit(solution)/shard_map/ppermute | solution.py:530
  123.3 66.8 %collective-permute-start.4 = (bf16[512,768]{1,0:T(8,128)(2,1)S(1)}, bf16[512,768]{1,0:T(8,128)(2,1)}, u32[]{:S(2)}, u32[]{:S(2)}) collective-permute-start(bf16[512,768]{1,0:T(8,128)(2,1)S(1)} %add_convert_fusion.8), channel_id=1, source_target_pairs={{0,2},{1,3},{2,0},{3,1},{4,6},{5,7},{6,4},{7,5},{8,10},{9,11},{10,... | collective-permute-start | bytes 2359304 | tf_op jit(solution)/shard_map/ppermute | solution.py:530
  145.9 46.2 %collective-permute-start.14 = (bf16[512,768]{1,0:T(8,128)(2,1)}, bf16[512,768]{1,0:T(8,128)(2,1)}, u32[]{:S(2)}, u32[]{:S(2)}) collective-permute-start(bf16[512,768]{1,0:T(8,128)(2,1)} %get-tuple-element.105.own_in), channel_id=1, source_target_pairs={{0,1},{1,0},{2,3},{3,2},{4,5},{5,4},{6,7},{7,6},{8,9},{9,8},{10,11... | collective-permute-start | bytes 2359304 | tf_op jit(solution)/shard_map/ppermute | solution.py:600
  157.7 32.3 %copy-start.2 = (f32[512,768]{1,0:T(8,128)S(1)}, f32[512,768]{1,0:T(8,128)}, u32[]{:S(2)}) copy-start(f32[512,768]{1,0:T(8,128)} %get-tuple-element.88.hidden_ref) | copy-start | bytes 4718596
  157.7 32.3 %copy-start.3 = (f32[512,768]{1,0:T(8,128)S(1)}, f32[512,768]{1,0:T(8,128)}, u32[]{:S(2)}) copy-start(f32[512,768]{1,0:T(8,128)} %get-tuple-element.97.hidden_ref) | copy-start | bytes 4718596
  157.7 32.3 %copy-start.37 = (f32[768]{0:T(1024)S(1)}, f32[768]{0:T(1024)}, u32[]{:S(2)}) copy-start(f32[768]{0:T(1024)} %param.33) | copy-start | bytes 9220
  163.2 60.6 %collective-permute-start.20 = (bf16[512,768]{1,0:T(8,128)(2,1)}, bf16[512,768]{1,0:T(8,128)(2,1)S(1)}, u32[]{:S(2)}, u32[]{:S(2)}) collective-permute-start(bf16[512,768]{1,0:T(8,128)(2,1)} %get-tuple-element.115.own_in), channel_id=1, source_target_pairs={{0,1},{1,0},{2,3},{3,2},{4,5},{5,4},{6,7},{7,6},{8,9},{9,8},{10,11... | collective-permute-start | bytes 2359304 | tf_op jit(solution)/shard_map/ppermute | solution.py:600
  192.0 53.8 %collective-permute-start.5 = (bf16[512,768]{1,0:T(8,128)(2,1)S(1)}, bf16[512,768]{1,0:T(8,128)(2,1)}, u32[]{:S(2)}, u32[]{:S(2)}) collective-permute-start(bf16[512,768]{1,0:T(8,128)(2,1)S(1)} %get-tuple-element.194), channel_id=1, source_target_pairs={{0,1},{1,0},{2,3},{3,2},{4,5},{5,4},{6,7},{7,6},{8,9},{9,8},{10,11... | collective-permute-start | bytes 2359304 | tf_op jit(solution)/shard_map/ppermute | solution.py:533
  210.3 38.1 %collective-permute-start.15 = (bf16[512,768]{1,0:T(8,128)(2,1)}, bf16[512,768]{1,0:T(8,128)(2,1)}, u32[]{:S(2)}, u32[]{:S(2)}) collective-permute-start(bf16[512,768]{1,0:T(8,128)(2,1)} %get-tuple-element.108), channel_id=1, source_target_pairs={{0,1},{1,0},{2,3},{3,2},{4,5},{5,4},{6,7},{7,6},{8,9},{9,8},{10,11... | collective-permute-start | bytes 2359304 | tf_op jit(solution)/shard_map/ppermute | solution.py:529
  224.6 19.2 %copy-start.41 = (f32[1,768]{1,0:T(1,128)S(1)}, f32[1,768]{1,0:T(1,128)}, u32[]{:S(2)}) copy-start(f32[1,768]{1,0:T(1,128)} %get-tuple-element.132) | copy-start | bytes 9220
  224.6 19.2 %copy-start.42 = (f32[1,768]{1,0:T(1,128)S(1)}, f32[1,768]{1,0:T(1,128)}, u32[]{:S(2)}) copy-start(f32[1,768]{1,0:T(1,128)} %get-tuple-element.134) | copy-start | bytes 9220
  224.7 19.2 %copy-start.43 = (f32[1,768]{1,0:T(1,128)S(1)}, f32[1,768]{1,0:T(1,128)}, u32[]{:S(2)}) copy-start(f32[1,768]{1,0:T(1,128)} %get-tuple-element.133) | copy-start | bytes 9220
  224.7 19.2 %copy-start.44 = (f32[1,768]{1,0:T(1,128)S(1)}, f32[1,768]{1,0:T(1,128)}, u32[]{:S(2)}) copy-start(f32[1,768]{1,0:T(1,128)} %get-tuple-element.131) | copy-start | bytes 9220
  224.7 19.7 %copy-start.34 = (f32[3,768]{1,0:T(4,128)S(1)}, f32[3,768]{1,0:T(4,128)}, u32[]{:S(2)}) copy-start(f32[3,768]{1,0:T(4,128)} %get-tuple-element.129) | copy-start | bytes 27652
  224.7 19.7 %copy-start.35 = (f32[3,768]{1,0:T(4,128)S(1)}, f32[3,768]{1,0:T(4,128)}, u32[]{:S(2)}) copy-start(f32[3,768]{1,0:T(4,128)} %get-tuple-element.130) | copy-start | bytes 27652
  243.8 10.4 %collective-permute-start.21 = (bf16[512,768]{1,0:T(8,128)(2,1)}, bf16[512,768]{1,0:T(8,128)(2,1)S(1)}, u32[]{:S(2)}, u32[]{:S(2)}) collective-permute-start(bf16[512,768]{1,0:T(8,128)(2,1)} %get-tuple-element.122), channel_id=1, source_target_pairs={{0,1},{1,0},{2,3},{3,2},{4,5},{5,4},{6,7},{7,6},{8,9},{9,8},{10,11... | collective-permute-start | bytes 2359304 | tf_op jit(solution)/shard_map/ppermute | solution.py:529
  243.9 10.6 %collective-permute-start.11 = (bf16[512,768]{1,0:T(8,128)(2,1)S(1)}, bf16[512,768]{1,0:T(8,128)(2,1)}, u32[]{:S(2)}, u32[]{:S(2)}) collective-permute-start(bf16[512,768]{1,0:T(8,128)(2,1)S(1)} %get-tuple-element.195), channel_id=1, source_target_pairs={{0,1},{1,0},{2,3},{3,2},{4,5},{5,4},{6,7},{7,6},{8,9},{9,8},{10,11... | collective-permute-start | bytes 2359304 | tf_op jit(solution)/shard_map/ppermute | solution.py:533
  244.4 17.0 %collective-permute-start.24 = (bf16[1024,192]{1,0:T(8,128)(2,1)}, bf16[1024,192]{1,0:T(8,128)(2,1)}, u32[]{:S(2)}, u32[]{:S(2)}) collective-permute-start(bf16[1024,192]{1,0:T(8,128)(2,1)} %get-tuple-element.125), channel_id=1, source_target_pairs={{2,0},{3,1},{6,4},{7,5},{10,8},{11,9},{14,12},{15,13},{18,16},{19,... | collective-permute-start | bytes 1179656 | tf_op jit(solution)/shard_map/ppermute | solution.py:633
  245.8 2.7 copy-start.20
  245.8 66.6 %collective-permute-start.26 = (bf16[1024,192]{1,0:T(8,128)(2,1)}, bf16[1024,192]{1,0:T(8,128)(2,1)}, u32[]{:S(2)}, u32[]{:S(2)}) collective-permute-start(bf16[1024,192]{1,0:T(8,128)(2,1)} %get-tuple-element.126), channel_id=1, source_target_pairs={{2,0},{3,1},{6,4},{7,5},{10,8},{11,9},{14,12},{15,13},{18,16},{19,... | collective-permute-start | bytes 1179656 | tf_op jit(solution)/shard_map/ppermute | solution.py:633
  248.4 5.8 %copy-start.21 = (bf16[512,768]{1,0:T(8,128)(2,1)S(1)}, bf16[512,768]{1,0:T(8,128)(2,1)}, u32[]{:S(2)}) copy-start(bf16[512,768]{1,0:T(8,128)(2,1)} %get-tuple-element.121) | copy-start | bytes 2359300
  249.9 6.2 %copy-start.5 = (bf16[512,768]{1,0:T(8,128)(2,1)}, bf16[512,768]{1,0:T(8,128)(2,1)S(1)}, u32[]{:S(2)}) copy-start(bf16[512,768]{1,0:T(8,128)(2,1)S(1)} %add_convert_fusion.2.part_ref) | copy-start | bytes 2359300
  249.9 39.5 %collective-permute-start.16 = (bf16[512,768]{1,0:T(8,128)(2,1)S(1)}, bf16[512,768]{1,0:T(8,128)(2,1)S(1)}, u32[]{:S(2)}, u32[]{:S(2)}) collective-permute-start(bf16[512,768]{1,0:T(8,128)(2,1)S(1)} %add_convert_fusion.2.part_ref), channel_id=1, source_target_pairs={{0,2},{1,3},{2,0},{3,1},{4,6},{5,7},{6,4},{7,5},{8,10},{9,11},{10,... | collective-permute-start | bytes 2359304 | tf_op jit(solution)/shard_map/ppermute | solution.py:530
  254.4 50.9 %collective-permute-start.22 = (bf16[512,768]{1,0:T(8,128)(2,1)S(1)}, bf16[512,768]{1,0:T(8,128)(2,1)S(1)}, u32[]{:S(2)}, u32[]{:S(2)}) collective-permute-start(bf16[512,768]{1,0:T(8,128)(2,1)S(1)} %add_convert_fusion.part_ref), channel_id=1, source_target_pairs={{0,2},{1,3},{2,0},{3,1},{4,6},{5,7},{6,4},{7,5},{8,10},{9,11},{10,... | collective-permute-start | bytes 2359304 | tf_op jit(solution)/shard_map/ppermute | solution.py:530
  262.5 54.1 %collective-permute-start.25 = (bf16[1024,192]{1,0:T(8,128)(2,1)S(1)}, bf16[1024,192]{1,0:T(8,128)(2,1)S(1)}, u32[]{:S(2)}, u32[]{:S(2)}) collective-permute-start(bf16[1024,192]{1,0:T(8,128)(2,1)S(1)} %broadcast_select_fusion.9), channel_id=1, source_target_pairs={{0,1},{1,0},{2,3},{3,2},{4,5},{5,4},{6,7},{7,6},{8,9},{9,8},{10,11... | collective-permute-start | bytes 1179656 | tf_op jit(solution)/shard_map/ppermute | solution.py:637
  306.2 4.8 %copy-start.36 = (f32[2,768]{1,0:T(2,128)S(1)}, f32[2,768]{1,0:T(2,128)}, u32[]{:S(2)}) copy-start(f32[2,768]{1,0:T(2,128)} %get-tuple-element.127) | copy-start | bytes 18436
  306.2 5.6 %copy-start.12 = (f32[512,768]{1,0:T(8,128)S(1)}, f32[512,768]{1,0:T(8,128)}, u32[]{:S(2)}) copy-start(f32[512,768]{1,0:T(8,128)} %get-tuple-element.110) | copy-start | bytes 4718596
  311.8 2.3 collective-permute-start.28
  311.8 16.5 %collective-permute-start.17 = (f32[512,768]{1,0:T(8,128)S(1)}, f32[512,768]{1,0:T(8,128)S(1)}, u32[]{:S(2)}, u32[]{:S(2)}) collective-permute-start(f32[512,768]{1,0:T(8,128)S(1)} %copy-done.12), channel_id=1, source_target_pairs={{0,1},{1,0},{2,3},{3,2},{4,5},{5,4},{6,7},{7,6},{8,9},{9,8},{10,11... | collective-permute-start | bytes 4718600 | tf_op jit(solution)/shard_map/ppermute | solution.py:533
  313.5 7.2 %collective-permute-start.27 = (bf16[1024,192]{1,0:T(8,128)(2,1)S(1)}, bf16[1024,192]{1,0:T(8,128)(2,1)S(1)}, u32[]{:S(2)}, u32[]{:S(2)}) collective-permute-start(bf16[1024,192]{1,0:T(8,128)(2,1)S(1)} %broadcast_select_fusion.8), channel_id=1, source_target_pairs={{0,1},{1,0},{2,3},{3,2},{4,5},{5,4},{6,7},{7,6},{8,9},{9,8},{10,11... | collective-permute-start | bytes 1179656 | tf_op jit(solution)/shard_map/ppermute | solution.py:637
  313.6 87.5 %collective-permute-start.23 = (f32[512,768]{1,0:T(8,128)}, f32[512,768]{1,0:T(8,128)}, u32[]{:S(2)}, u32[]{:S(2)}) collective-permute-start(f32[512,768]{1,0:T(8,128)} %get-tuple-element.124), channel_id=1, source_target_pairs={{0,1},{1,0},{2,3},{3,2},{4,5},{5,4},{6,7},{7,6},{8,9},{9,8},{10,11... | collective-permute-start | bytes 4718600 | tf_op jit(solution)/shard_map/ppermute | solution.py:533
  314.1 4.4 %collective-permute-start.29 = (f32[6,768]{1,0:T(8,128)S(1)}, f32[6,768]{1,0:T(8,128)S(1)}, u32[]{:S(2)}, u32[]{:S(2)}) collective-permute-start(f32[6,768]{1,0:T(8,128)S(1)} %pad_maximum_fusion.3), channel_id=1, source_target_pairs={{0,4},{4,0},{8,12},{12,8},{16,20},{20,16},{24,28},{28,24},{1,5},{5... | collective-permute-start | bytes 55304 | tf_op jit(solution)/shard_map/ppermute | solution.py:484
  318.5 4.1 collective-permute-start.30
  322.5 5.1 %collective-permute-start.31 = (f32[6,768]{1,0:T(8,128)S(1)}, f32[6,768]{1,0:T(8,128)S(1)}, u32[]{:S(2)}, u32[]{:S(2)}) collective-permute-start(f32[6,768]{1,0:T(8,128)S(1)} %add.122), channel_id=1, source_target_pairs={{0,16},{4,20},{8,24},{12,28},{16,0},{20,4},{24,8},{28,12},{1,17},{... | collective-permute-start | bytes 55304 | tf_op jit(solution)/shard_map/ppermute | solution.py:484
  397.5 12.0 %copy-start.31 = (bf16[768,192]{1,0:T(8,128)(2,1)S(1)}, bf16[768,192]{1,0:T(8,128)(2,1)}, u32[]{:S(2)}) copy-start(bf16[768,192]{1,0:T(8,128)(2,1)} %get-tuple-element.174) | copy-start | bytes 884740
  397.5 12.0 %collective-permute-start.32 = (bf16[768,192]{1,0:T(8,128)(2,1)}, bf16[768,192]{1,0:T(8,128)(2,1)S(1)}, u32[]{:S(2)}, u32[]{:S(2)}) collective-permute-start(bf16[768,192]{1,0:T(8,128)(2,1)} %get-tuple-element.174), channel_id=1, source_target_pairs={{0,2},{1,3},{4,6},{5,7},{8,10},{9,11},{12,14},{13,15},{16,18},{17,... | collective-permute-start | bytes 884744 | tf_op jit(solution)/shard_map/ppermute | solution.py:646
  409.6 9.1 %collective-permute-start.33 = (bf16[768,192]{1,0:T(8,128)(2,1)S(1)}, bf16[768,192]{1,0:T(8,128)(2,1)}, u32[]{:S(2)}, u32[]{:S(2)}) collective-permute-start(bf16[768,192]{1,0:T(8,128)(2,1)S(1)} %broadcast_select_fusion.16), channel_id=1, source_target_pairs={{0,1},{1,0},{2,3},{3,2},{4,5},{5,4},{6,7},{7,6},{8,9},{9,8},{10,11... | collective-permute-start | bytes 884744 | tf_op jit(solution)/shard_map/ppermute | solution.py:648
  409.7 2.9 copy-start.14
  417.7 3.2 copy-start.1
  (17 other events, 24.6 us)
Sparse Core Ops, SparseCore 0:
  245.9 151.6 all-reduce.2
